TPU v7x, 32 devices: a whole 2x2x4 slice. The times are simulated.
32 devices in a mesh: gx: 8 (over y, x, core), gy: 4 (over z).
Axes of the slice: x: 2, y: 2, z: 4, core: 2. Of those that a mesh axis runs over, the one named last changes fastest.
Arguments:
- value_field: float32 [32, 32, 8, 1024], P('gx', 'gy'), may hold values from -6 to 6
- obstacle: float32 [32, 32, 8, 1024], P('gx', 'gy'), may hold values from -4 to 4
- drift_field: float32 [32, 32, 2], P('gx', 'gy'), may hold values from -9 to 9
Outputs:
- value_next: float32 [32, 32, 8, 1024], P('gx', 'gy')
- steps_taken: float32 [4], replicated
All inputs are finite; a program needn't handle non-finite values.
Results may differ from a plain program's by a relative error of at most 0.00002.
Values sent between devices are 32-bit elements; how exact they have to be, the bound alone decides.
No kernel may reach another device: no remote copies, remote signals or barrier semaphores. Data moves between devices by JAX's collectives and lax.ppermute only.
A program may use at most 128 MiB of HBM per device.

v0:
```python
import math

import jax
import jax.numpy as jnp
from jax import lax
from jax.sharding import PartitionSpec as P

NTH = 8
NV = 16
NW = 64
ITERS = 4


SPACE_STEP = 0.5
SPEED_BASE = 1.0
SPEED_STEP = 0.2
TURN_LIMIT = 0.25
EFFORT_COST = 10.0
COURANT = 0.9


def with_halo(cells, sides, width):
    for axis, dim in sides:
        count = lax.axis_size(axis)
        ends = count - 1
        head = lax.slice_in_dim(cells, 0, width, axis=dim)
        tail = lax.slice_in_dim(cells, cells.shape[dim] - width, cells.shape[dim], axis=dim)
        cells = jnp.concatenate(
            [
                lax.ppermute(tail, axis, [(i, (i + 1) % count) for i in range(ends)]),
                cells,
                lax.ppermute(head, axis, [((i + 1) % count, i) for i in range(ends)]),
            ],
            axis=dim,
        )
    return cells


def grid_lanes():
    heading = jnp.arange(NTH, dtype=jnp.int32).astype(jnp.float32) * (2.0 * math.pi / NTH)
    lane_index = jnp.arange(NV * NW, dtype=jnp.int32)
    speed_row = SPEED_BASE + (lane_index // NW).astype(jnp.float32) * SPEED_STEP
    turning = -1.0 + ((lane_index % NW).astype(jnp.float32) + 0.5) * (2.0 / NW)
    cosine_speed = jnp.cos(heading)[:, None] * speed_row[None, :]
    sine_speed = jnp.sin(heading)[:, None] * speed_row[None, :]
    return (cosine_speed, sine_speed, turning)


def rate_field(drift_part):
    cosine_speed, sine_speed, turning = grid_lanes()
    east_rate = cosine_speed + drift_part[:, :, 0][:, :, None, None]
    north_rate = sine_speed + drift_part[:, :, 1][:, :, None, None]
    head_step = 2.0 * math.pi / NTH
    turn_step = 2.0 / NW
    return (
        jnp.abs(east_rate) / SPACE_STEP
        + jnp.abs(north_rate) / SPACE_STEP
        + jnp.abs(turning) / head_step
        + TURN_LIMIT / turn_step
    )


def advance(extended, drift_part, barrier, time_step, slope_rate):
    center = extended[1:-1, 1:-1]
    east_plus = (extended[2:, 1:-1] - center) / SPACE_STEP
    east_minus = (center - extended[:-2, 1:-1]) / SPACE_STEP
    north_plus = (extended[1:-1, 2:] - center) / SPACE_STEP
    north_minus = (center - extended[1:-1, :-2]) / SPACE_STEP
    head_step = 2.0 * math.pi / NTH
    turn_step = 2.0 / NW
    head_plus = (jnp.roll(center, -1, axis=2) - center) / head_step
    head_minus = (center - jnp.roll(center, 1, axis=2)) / head_step
    speed_diff = (center[..., NW:] - center[..., :-NW]) / SPEED_STEP
    speed_plus = jnp.concatenate([speed_diff, speed_diff[..., -NW:]], axis=3)
    speed_minus = jnp.concatenate([speed_diff[..., :NW], speed_diff], axis=3)
    turn_diff = (center[..., 1:] - center[..., :-1]) / turn_step
    padding = jnp.zeros_like(turn_diff[..., :1])
    forward = jnp.concatenate([turn_diff, padding], axis=3)
    backward = jnp.concatenate([padding, turn_diff], axis=3)
    lane_pos = jnp.arange(center.shape[3], dtype=jnp.int32) % NW
    turn_plus = jnp.where(lane_pos == NW - 1, backward, forward)
    turn_minus = jnp.where(lane_pos == 0, forward, backward)
    cosine_speed, sine_speed, turning = grid_lanes()
    east_rate = cosine_speed + drift_part[:, :, 0][:, :, None, None]
    north_rate = sine_speed + drift_part[:, :, 1][:, :, None, None]
    speed_mean = 0.5 * (speed_plus + speed_minus)
    hamiltonian = (
        east_rate * (0.5 * (east_plus + east_minus))
        + north_rate * (0.5 * (north_plus + north_minus))
        + turning * (0.5 * (head_plus + head_minus))
        + speed_mean * speed_mean / (2.0 * EFFORT_COST)
        + TURN_LIMIT * jnp.abs(0.5 * (turn_plus + turn_minus))
    )
    damping = (
        jnp.abs(east_rate) * (0.5 * (east_plus - east_minus))
        + jnp.abs(north_rate) * (0.5 * (north_plus - north_minus))
        + jnp.abs(turning) * (0.5 * (head_plus - head_minus))
        + slope_rate * (0.5 * (speed_plus - speed_minus))
        + TURN_LIMIT * (0.5 * (turn_plus - turn_minus))
    )
    return jnp.minimum(center + time_step * (hamiltonian + damping), barrier)


def edge_fill(extended, width, low_x, high_x, low_y, high_y):
    inner_x = extended.shape[0] - 2 * width
    inner_y = extended.shape[1] - 2 * width
    left_rim = jnp.where(low_x, 2.0 * extended[width] - extended[width + 1], extended[width - 1])
    extended = extended.at[width - 1].set(left_rim)
    right_at = width + inner_x
    right_rim = jnp.where(
        high_x, 2.0 * extended[right_at - 1] - extended[right_at - 2], extended[right_at]
    )
    extended = extended.at[right_at].set(right_rim)
    lower_rim = jnp.where(
        low_y, 2.0 * extended[:, width] - extended[:, width + 1], extended[:, width - 1]
    )
    extended = extended.at[:, width - 1].set(lower_rim)
    top_at = width + inner_y
    upper_rim = jnp.where(
        high_y, 2.0 * extended[:, top_at - 1] - extended[:, top_at - 2], extended[:, top_at]
    )
    extended = extended.at[:, top_at].set(upper_rim)
    return extended


def per_device(value_field, obstacle, drift_field):
    low_x = lax.axis_index("gx") == 0
    high_x = lax.axis_index("gx") == lax.axis_size("gx") - 1
    low_y = lax.axis_index("gy") == 0
    high_y = lax.axis_index("gy") == lax.axis_size("gy") - 1
    rate_cells = rate_field(drift_field)
    rate_top = None
    step_list = []
    current_value = value_field
    for step_index in range(ITERS):
        extended = with_halo(current_value, (("gx", 0), ("gy", 1)), 1)
        step_rate_top = rate_top
        local_slope = jnp.max(jnp.abs(current_value[..., NW:] - current_value[..., :-NW]))
        if step_index == 0:
            slope_peak, step_rate_top = lax.pmax((local_slope, jnp.max(rate_cells)), ("gx", "gy"))
        else:
            slope_peak = lax.pmax(local_slope, ("gx", "gy"))
        top_slope = slope_peak / SPEED_STEP
        rate_bound = step_rate_top + top_slope / (EFFORT_COST * SPEED_STEP)
        time_step = COURANT / rate_bound
        slope_rate = top_slope / EFFORT_COST
        rate_top = step_rate_top
        step_list.append(time_step)
        current_value = advance(
            edge_fill(extended, 1, low_x, high_x, low_y, high_y),
            drift_field,
            obstacle,
            time_step,
            slope_rate,
        )
    return (current_value, jnp.stack(step_list))


def solution(mesh):
    return jax.shard_map(
        per_device,
        mesh=mesh,
        in_specs=(P("gx", "gy", None, None), P("gx", "gy", None, None), P("gx", "gy", None)),
        out_specs=(P("gx", "gy", None, None), P()),
        check_vma=False,
    )
```

profile of v0, /device:TPU:0, one launch (start us, length us, event | category | flops | bytes accessed | tf_op | source)
XLA Modules:
  0.0 264.4 jit_solution(4856829526070138169)
XLA Ops:
  0.6 1.2 fusion.153
  1.8 1.3 collective-permute-start.1
  3.1 3.0 %collective-permute-start = (f32[1,8,8,1024]{3,2,1,0:T(8,128)S(1)}, f32[1,8,8,1024]{3,2,1,0:T(8,128)S(1)}, u32[]{:S(2)}, u32[]{:S(2)}) collective-permute-start(f32[1,8,8,1024]{3,2,1,0:T(8,128)S(1)} %get-tuple-element.235), channel_id=1, source_target_pairs={{0,4},{4,8},{8,12},{12,16},{16,20},{20,24},{24,28},{1,5},{5,9},{9,... | collective-permute-start | bytes 786440 | tf_op jit(solution)/shard_map/ppermute | solution.py:30
  7.1 1.0 fusion.44
  9.0 42.6 %all-reduce.8 = (f32[]{:T(128)}, f32[]{:T(128)}) all-reduce(f32[]{:T(128)} %abs_reduce_fusion, f32[]{:T(128)} %fusion.44), channel_id=1, replica_groups=mesh['gx'=8,'gy'=4] {'gx','gy'}, use_global_device_ids=true, to_apply=%region_3.4 | all-reduce | flops 2 | bytes 16 | tf_op jit(solution)/shard_map/pmax | solution.py:140
  53.8 3.4 %collective-permute-start.2 = (f32[6,1,8,1024]{3,2,1,0:T(8,128)S(1)}, f32[6,1,8,1024]{3,2,1,0:T(8,128)S(1)}, u32[]{:S(2)}, u32[]{:S(2)}) collective-permute-start(f32[6,1,8,1024]{3,2,1,0:T(8,128)S(1)} %get-tuple-element.218), channel_id=1, source_target_pairs={{0,1},{1,2},{2,3},{4,5},{5,6},{6,7},{8,9},{9,10},{10,11},{12,13},{... | collective-permute-start | bytes 589832 | tf_op jit(solution)/shard_map/ppermute | solution.py:30
  57.3 1.3 collective-permute-start.3
  58.6 2.2 collective-permute-done.2
  60.8 4.1 %collective-permute-done.3 = f32[6,1,8,1024]{3,2,1,0:T(8,128)S(1)} collective-permute-done((f32[6,1,8,1024]{3,2,1,0:T(8,128)S(1)}, f32[6,1,8,1024]{3,2,1,0:T(8,128)S(1)}, u32[]{:S(2)}, u32[]{:S(2)}) %collective-permute-start.3) | collective-permute-done | bytes 196640 | tf_op jit(solution)/shard_map/ppermute | solution.py:32
  67.6 2.7 %fusion.16 = f32[4,8,8,1024]{3,2,1,0:T(8,128)S(1)} fusion(f32[4,8,8,1024]{3,2,1,0:T(8,128)S(1)} %copy-done, f32[4,8,8,1023]{3,2,1,0:T(8,128)S(1)} %fusion.85, f32[4,8,8,960]{3,2,1,0:T(8,128)S(1)} %fusion.86, f32[4,8,8,64]{3,2,1,0:T(8,128)S(1)} %get-tuple-element.233, f32[4,8,8,64]{3,2,1,0:T(8,128)S(1)} %get-tuple-element.232, ...), kind=kLoop, calls=%fused_computation.30 | loop fusion | flops 16252928 | bytes 11674888 | tf_op jit(solution)/shard_map/min | solution.py:101
  70.4 1.3 collective-permute-start.4
  71.7 1.3 collective-permute-start.5
  73.0 4.6 %collective-permute-done.5 = f32[1,8,8,1024]{3,2,1,0:T(8,128)S(1)} collective-permute-done((f32[1,8,8,1024]{3,2,1,0:T(8,128)S(1)}, f32[1,8,8,1024]{3,2,1,0:T(8,128)S(1)}, u32[]{:S(2)}, u32[]{:S(2)}) %collective-permute-start.5) | collective-permute-done | bytes 262176 | tf_op jit(solution)/shard_map/ppermute | solution.py:32
  77.6 3.3 %collective-permute-start.6 = (f32[6,1,8,1024]{3,2,1,0:T(8,128)S(1)}, f32[6,1,8,1024]{3,2,1,0:T(8,128)S(1)}, u32[]{:S(2)}, u32[]{:S(2)}) collective-permute-start(f32[6,1,8,1024]{3,2,1,0:T(8,128)S(1)} %get-tuple-element.216), channel_id=1, source_target_pairs={{0,1},{1,2},{2,3},{4,5},{5,6},{6,7},{8,9},{9,10},{10,11},{12,13},{... | collective-permute-start | bytes 589832 | tf_op jit(solution)/shard_map/ppermute | solution.py:30
  80.9 1.3 collective-permute-start.7
  82.2 1.0 fusion.84
  83.2 45.2 %pmax.37 = f32[]{:T(128)} all-reduce(f32[]{:T(128)} %fusion.84), channel_id=1, replica_groups=mesh['gx'=8,'gy'=4] {'gx','gy'}, use_global_device_ids=true, to_apply=%region_5.6 | all-reduce | flops 1 | bytes 8 | tf_op jit(solution)/shard_map/pmax | solution.py:142
  132.2 2.8 %fusion.24 = f32[4,8,8,1024]{3,2,1,0:T(8,128)S(1)} fusion(f32[4,8,8,1024]{3,2,1,0:T(8,128)S(1)} %copy-done, f32[4,8,8,1023]{3,2,1,0:T(8,128)S(1)} %fusion.77, f32[4,8,8,960]{3,2,1,0:T(8,128)S(1)} %fusion.78, f32[4,8,8,64]{3,2,1,0:T(8,128)S(1)} %get-tuple-element.229, f32[4,8,8,64]{3,2,1,0:T(8,128)S(1)} %get-tuple-element.228, ...), kind=kLoop, calls=%fused_computation.38 | loop fusion | flops 16252928 | bytes 11674888 | tf_op jit(solution)/shard_map/min | solution.py:101
  135.0 1.3 collective-permute-start.8
  136.3 1.3 collective-permute-start.9
  137.6 4.6 %collective-permute-done.9 = f32[1,8,8,1024]{3,2,1,0:T(8,128)S(1)} collective-permute-done((f32[1,8,8,1024]{3,2,1,0:T(8,128)S(1)}, f32[1,8,8,1024]{3,2,1,0:T(8,128)S(1)}, u32[]{:S(2)}, u32[]{:S(2)}) %collective-permute-start.9) | collective-permute-done | bytes 262176 | tf_op jit(solution)/shard_map/ppermute | solution.py:32
  142.3 1.8 collective-permute-start.10
  144.2 1.3 collective-permute-start.11
  146.4 45.4 %pmax.38 = f32[]{:T(128)} all-reduce(f32[]{:T(128)} %fusion.76), channel_id=1, replica_groups=mesh['gx'=8,'gy'=4] {'gx','gy'}, use_global_device_ids=true, to_apply=%region_7.8 | all-reduce | flops 1 | bytes 8 | tf_op jit(solution)/shard_map/pmax | solution.py:142
  195.6 2.8 %fusion.32 = f32[4,8,8,1024]{3,2,1,0:T(8,128)S(1)} fusion(f32[4,8,8,1024]{3,2,1,0:T(8,128)S(1)} %copy-done, f32[4,8,8,1023]{3,2,1,0:T(8,128)S(1)} %fusion.69, f32[4,8,8,960]{3,2,1,0:T(8,128)S(1)} %fusion.70, f32[4,8,8,64]{3,2,1,0:T(8,128)S(1)} %get-tuple-element.225, f32[4,8,8,64]{3,2,1,0:T(8,128)S(1)} %get-tuple-element.224, ...), kind=kLoop, calls=%fused_computation.46 | loop fusion | flops 16252928 | bytes 11674888 | tf_op jit(solution)/shard_map/min | solution.py:101
  198.4 1.3 collective-permute-start.12
  199.7 1.3 collective-permute-start.13
  201.1 4.6 %collective-permute-done.13 = f32[1,8,8,1024]{3,2,1,0:T(8,128)S(1)} collective-permute-done((f32[1,8,8,1024]{3,2,1,0:T(8,128)S(1)}, f32[1,8,8,1024]{3,2,1,0:T(8,128)S(1)}, u32[]{:S(2)}, u32[]{:S(2)}) %collective-permute-start.13) | collective-permute-done | bytes 262176 | tf_op jit(solution)/shard_map/ppermute | solution.py:32
  205.7 3.3 %collective-permute-start.14 = (f32[6,1,8,1024]{3,2,1,0:T(8,128)S(1)}, f32[6,1,8,1024]{3,2,1,0:T(8,128)S(1)}, u32[]{:S(2)}, u32[]{:S(2)}) collective-permute-start(f32[6,1,8,1024]{3,2,1,0:T(8,128)S(1)} %get-tuple-element.212), channel_id=1, source_target_pairs={{0,1},{1,2},{2,3},{4,5},{5,6},{6,7},{8,9},{9,10},{10,11},{12,13},{... | collective-permute-start | bytes 589832 | tf_op jit(solution)/shard_map/ppermute | solution.py:30
  209.0 1.3 collective-permute-start.15
  211.2 45.2 %pmax.39 = f32[]{:T(128)} all-reduce(f32[]{:T(128)} %fusion.68), channel_id=1, replica_groups=mesh['gx'=8,'gy'=4] {'gx','gy'}, use_global_device_ids=true, to_apply=%region_9.10 | all-reduce | flops 1 | bytes 8 | tf_op jit(solution)/shard_map/pmax | solution.py:142
  260.8 3.5 %fusion.40 = f32[4,8,8,1024]{3,2,1,0:T(8,128)} fusion(f32[4,8,8,1024]{3,2,1,0:T(8,128)S(1)} %copy-done, f32[4,8,8,1023]{3,2,1,0:T(8,128)S(1)} %fusion.61, f32[4,8,8,960]{3,2,1,0:T(8,128)S(1)} %fusion.62, f32[4,8,8,64]{3,2,1,0:T(8,128)S(1)} %get-tuple-element.221, f32[4,8,8,64]{3,2,1,0:T(8,128)S(1)} %get-tuple-element.220, ...), kind=kLoop, calls=%fused_computation.54 | loop fusion | flops 16252928 | bytes 11674888 | tf_op jit(solution)/shard_map/min | solution.py:101
  (91 shorter events, 12.5 us)
Async XLA Ops:
  0.6 7.4 %copy-start.1 = (f32[4,8,8,1024]{3,2,1,0:T(8,128)S(1)}, f32[4,8,8,1024]{3,2,1,0:T(8,128)}, u32[]{:S(2)}) copy-start(f32[4,8,8,1024]{3,2,1,0:T(8,128)} %param.35) | copy-start | bytes 3145732
  1.8 52.0 %collective-permute-start.1 = (f32[1,8,8,1024]{3,2,1,0:T(8,128)S(1)}, f32[1,8,8,1024]{3,2,1,0:T(8,128)S(1)}, u32[]{:S(2)}, u32[]{:S(2)}) collective-permute-start(f32[1,8,8,1024]{3,2,1,0:T(8,128)S(1)} %get-tuple-element.234), channel_id=1, source_target_pairs={{4,0},{8,4},{12,8},{16,12},{20,16},{24,20},{28,24},{5,1},{9,5},{13... | collective-permute-start | bytes 786440 | tf_op jit(solution)/shard_map/ppermute | solution.py:32
  3.1 50.5 %collective-permute-start = (f32[1,8,8,1024]{3,2,1,0:T(8,128)S(1)}, f32[1,8,8,1024]{3,2,1,0:T(8,128)S(1)}, u32[]{:S(2)}, u32[]{:S(2)}) collective-permute-start(f32[1,8,8,1024]{3,2,1,0:T(8,128)S(1)} %get-tuple-element.235), channel_id=1, source_target_pairs={{0,4},{4,8},{8,12},{12,16},{16,20},{20,24},{24,28},{1,5},{5,9},{9,... | collective-permute-start | bytes 786440 | tf_op jit(solution)/shard_map/ppermute | solution.py:30
  53.8 6.9 %collective-permute-start.2 = (f32[6,1,8,1024]{3,2,1,0:T(8,128)S(1)}, f32[6,1,8,1024]{3,2,1,0:T(8,128)S(1)}, u32[]{:S(2)}, u32[]{:S(2)}) collective-permute-start(f32[6,1,8,1024]{3,2,1,0:T(8,128)S(1)} %get-tuple-element.218), channel_id=1, source_target_pairs={{0,1},{1,2},{2,3},{4,5},{5,6},{6,7},{8,9},{9,10},{10,11},{12,13},{... | collective-permute-start | bytes 589832 | tf_op jit(solution)/shard_map/ppermute | solution.py:30
  57.3 7.6 %collective-permute-start.3 = (f32[6,1,8,1024]{3,2,1,0:T(8,128)S(1)}, f32[6,1,8,1024]{3,2,1,0:T(8,128)S(1)}, u32[]{:S(2)}, u32[]{:S(2)}) collective-permute-start(f32[6,1,8,1024]{3,2,1,0:T(8,128)S(1)} %get-tuple-element.219), channel_id=1, source_target_pairs={{1,0},{2,1},{3,2},{5,4},{6,5},{7,6},{9,8},{10,9},{11,10},{13,12},{... | collective-permute-start | bytes 589832 | tf_op jit(solution)/shard_map/ppermute | solution.py:32
  66.4 1.2 copy-start
  70.4 2.6 collective-permute-start.4
  71.7 5.9 %collective-permute-start.5 = (f32[1,8,8,1024]{3,2,1,0:T(8,128)S(1)}, f32[1,8,8,1024]{3,2,1,0:T(8,128)S(1)}, u32[]{:S(2)}, u32[]{:S(2)}) collective-permute-start(f32[1,8,8,1024]{3,2,1,0:T(8,128)S(1)} %get-tuple-element.231), channel_id=1, source_target_pairs={{4,0},{8,4},{12,8},{16,12},{20,16},{24,20},{28,24},{5,1},{9,5},{13... | collective-permute-start | bytes 786440 | tf_op jit(solution)/shard_map/ppermute | solution.py:32
  77.6 52.8 %collective-permute-start.6 = (f32[6,1,8,1024]{3,2,1,0:T(8,128)S(1)}, f32[6,1,8,1024]{3,2,1,0:T(8,128)S(1)}, u32[]{:S(2)}, u32[]{:S(2)}) collective-permute-start(f32[6,1,8,1024]{3,2,1,0:T(8,128)S(1)} %get-tuple-element.216), channel_id=1, source_target_pairs={{0,1},{1,2},{2,3},{4,5},{5,6},{6,7},{8,9},{9,10},{10,11},{12,13},{... | collective-permute-start | bytes 589832 | tf_op jit(solution)/shard_map/ppermute | solution.py:30
  80.9 49.5 %collective-permute-start.7 = (f32[6,1,8,1024]{3,2,1,0:T(8,128)S(1)}, f32[6,1,8,1024]{3,2,1,0:T(8,128)S(1)}, u32[]{:S(2)}, u32[]{:S(2)}) collective-permute-start(f32[6,1,8,1024]{3,2,1,0:T(8,128)S(1)} %get-tuple-element.217), channel_id=1, source_target_pairs={{1,0},{2,1},{3,2},{5,4},{6,5},{7,6},{9,8},{10,9},{11,10},{13,12},{... | collective-permute-start | bytes 589832 | tf_op jit(solution)/shard_map/ppermute | solution.py:32
  135.0 2.6 collective-permute-start.8
  136.3 5.9 %collective-permute-start.9 = (f32[1,8,8,1024]{3,2,1,0:T(8,128)S(1)}, f32[1,8,8,1024]{3,2,1,0:T(8,128)S(1)}, u32[]{:S(2)}, u32[]{:S(2)}) collective-permute-start(f32[1,8,8,1024]{3,2,1,0:T(8,128)S(1)} %get-tuple-element.227), channel_id=1, source_target_pairs={{4,0},{8,4},{12,8},{16,12},{20,16},{24,20},{28,24},{5,1},{9,5},{13... | collective-permute-start | bytes 786440 | tf_op jit(solution)/shard_map/ppermute | solution.py:32
  142.3 51.5 %collective-permute-start.10 = (f32[6,1,8,1024]{3,2,1,0:T(8,128)S(1)}, f32[6,1,8,1024]{3,2,1,0:T(8,128)S(1)}, u32[]{:S(2)}, u32[]{:S(2)}) collective-permute-start(f32[6,1,8,1024]{3,2,1,0:T(8,128)S(1)} %get-tuple-element.214), channel_id=1, source_target_pairs={{0,1},{1,2},{2,3},{4,5},{5,6},{6,7},{8,9},{9,10},{10,11},{12,13},{... | collective-permute-start | bytes 589832 | tf_op jit(solution)/shard_map/ppermute | solution.py:30
  144.2 49.7 %collective-permute-start.11 = (f32[6,1,8,1024]{3,2,1,0:T(8,128)S(1)}, f32[6,1,8,1024]{3,2,1,0:T(8,128)S(1)}, u32[]{:S(2)}, u32[]{:S(2)}) collective-permute-start(f32[6,1,8,1024]{3,2,1,0:T(8,128)S(1)} %get-tuple-element.215), channel_id=1, source_target_pairs={{1,0},{2,1},{3,2},{5,4},{6,5},{7,6},{9,8},{10,9},{11,10},{13,12},{... | collective-permute-start | bytes 589832 | tf_op jit(solution)/shard_map/ppermute | solution.py:32
  198.4 2.6 collective-permute-start.12
  199.7 5.9 %collective-permute-start.13 = (f32[1,8,8,1024]{3,2,1,0:T(8,128)S(1)}, f32[1,8,8,1024]{3,2,1,0:T(8,128)S(1)}, u32[]{:S(2)}, u32[]{:S(2)}) collective-permute-start(f32[1,8,8,1024]{3,2,1,0:T(8,128)S(1)} %get-tuple-element.223), channel_id=1, source_target_pairs={{4,0},{8,4},{12,8},{16,12},{20,16},{24,20},{28,24},{5,1},{9,5},{13... | collective-permute-start | bytes 786440 | tf_op jit(solution)/shard_map/ppermute | solution.py:32
  205.7 53.4 %collective-permute-start.14 = (f32[6,1,8,1024]{3,2,1,0:T(8,128)S(1)}, f32[6,1,8,1024]{3,2,1,0:T(8,128)S(1)}, u32[]{:S(2)}, u32[]{:S(2)}) collective-permute-start(f32[6,1,8,1024]{3,2,1,0:T(8,128)S(1)} %get-tuple-element.212), channel_id=1, source_target_pairs={{0,1},{1,2},{2,3},{4,5},{5,6},{6,7},{8,9},{9,10},{10,11},{12,13},{... | collective-permute-start | bytes 589832 | tf_op jit(solution)/shard_map/ppermute | solution.py:30
  209.0 50.1 %collective-permute-start.15 = (f32[6,1,8,1024]{3,2,1,0:T(8,128)S(1)}, f32[6,1,8,1024]{3,2,1,0:T(8,128)S(1)}, u32[]{:S(2)}, u32[]{:S(2)}) collective-permute-start(f32[6,1,8,1024]{3,2,1,0:T(8,128)S(1)} %get-tuple-element.213), channel_id=1, source_target_pairs={{1,0},{2,1},{3,2},{5,4},{6,5},{7,6},{9,8},{10,9},{11,10},{13,12},{... | collective-permute-start | bytes 589832 | tf_op jit(solution)/shard_map/ppermute | solution.py:32
where the time goes:
time: 266 us; the launch traced here: 264 us
  blocking collectives  178 us (67%)
  starting transfers between devices  29.1 us (11%)
  other arithmetic  22.4 us (8%)
  waiting for transfers between devices  20.1 us (8%)
  between operations  9.32 us (4%)
  local copies, waits for them, and re-layouts  4.92 us (2%)
    pmax x3, blocking collectives, per_device(): slope_peak = lax.pmax(local_slope, ('gx', 'gy'))  136 us
    pmax x1, blocking collectives, per_device(): lax.pmax((local_slope, jnp.max(rate_cells)), ('gx', 'gy'))  42.6 us
    ppermute x8, starting transfers between devices, with_halo(): lax.ppermute(tail, axis, [(i, (i + 1) % count) for i in range(ends)])  18.8 us
    ppermute x8, waiting for transfers between devices, with_halo(): lax.ppermute(head, axis, [((i + 1) % count, i) for i in range(ends)])  17.9 us
    min x4, other arithmetic, advance(): return jnp.minimum(center + time_step * (hamiltonian + damping), barrier)  11.8 us
    ppermute x8, starting transfers between devices, with_halo(): lax.ppermute(head, axis, [((i + 1) % count, i) for i in range(ends)])  10.3 us
  transfers between devices with their start and end apart: 16, of which 5 were waited for; matrix products, arithmetic and copies ran while one was open for 2% of the time, Pallas kernels for 0%

commit v1 on v0

v1 whole, which is shorter than its diff:
```python
import functools
import math

import jax
import jax.numpy as jnp
import numpy as np
from jax import lax
from jax.experimental import pallas as pl
from jax.experimental.pallas import tpu as pltpu
from jax.sharding import PartitionSpec as P


NTH = 8
NV = 16
NW = 64
ITERS = 4

SPACE_STEP = 0.5
SPEED_BASE = 1.0
SPEED_STEP = 0.2
TURN_LIMIT = 0.25
EFFORT_COST = 10.0
COURANT = 0.9
HEAD_STEP = 2.0 * math.pi / NTH
TURN_STEP = 2.0 / NW

LANES = 128
TILE = (NTH, LANES)
SLABS = NV * NW // LANES
VMEM_LIMIT = 24 * 1024 * 1024


def iota(dim):
    return lax.broadcasted_iota(jnp.int32, TILE, dim)


def lanes(j):
    return slice(j * LANES, (j + 1) * LANES)


def half_turn(c):
    return pltpu.roll(c, LANES // 2, axis=1)


def load(ref, *at):
    return [ref[(*at, slice(None), lanes(j))] for j in range(SLABS)]


def store(ref, cells, *at):
    for j in range(SLABS):
        ref[(*at, slice(None), lanes(j))] = cells[j]


def apart(cells, low):
    middle = SLABS // 2
    out = []
    for below, above in zip(cells[:middle], cells[middle:]):
        out += [jnp.where(low, below, half_turn(above)), jnp.where(low, half_turn(below), above)]
    return out


def together(cells, low):
    below = [jnp.where(low, c, half_turn(d)) for c, d in zip(cells[::2], cells[1::2])]
    above = [jnp.where(low, half_turn(c), d) for c, d in zip(cells[::2], cells[1::2])]
    return below + above


def speed_gap(peak, cells, low):
    for j in range(SLABS - 1):
        peak = jnp.maximum(peak, jnp.abs(cells[j + 1] - cells[j]))
    seam = jnp.abs(half_turn(cells[0]) - cells[-1])
    return jnp.maximum(peak, jnp.where(low, seam, 0.0))


def speed_sides(cells, j, low, twice):
    if j < SLABS - 1:
        after = cells[j + 1]
    else:
        after = jnp.where(low, half_turn(cells[0]), twice - cells[j - 1])
    if j:
        before = cells[j - 1]
    else:
        before = jnp.where(low, twice - cells[1], half_turn(cells[-1]))
    return after, before


def wind_at(wind, x, y):
    return wind[0, x, pl.ds(y, 1), :], wind[1, x, pl.ds(y, 1), :]


def gap_row(peak, rate_row, low):
    return jnp.where(low[:1], jnp.max(peak, keepdims=True), rate_row)


def part_sizes(bx, by):
    sizes = [by, by, bx, bx]
    return sizes + [bx * by - sum(sizes)]


def runs(bx, by):
    out, at = [], 0
    for part, size in enumerate(part_sizes(bx, by)):
        done = 0
        while done < size:
            x, y = divmod(at, by)
            length = min(size - done, by - y)
            out.append((part, done, x, y, length))
            done, at = done + length, at + length
    return out


def walk(length, width, body, carry):
    width = math.gcd(length, width)

    def trip(t, carry):
        for i in range(width):
            carry = body(t * width + i, carry)
        return carry

    return lax.fori_loop(0, length // width, trip, carry)


def fill_edges(field, near, far, low_y, high_y):
    bx, by = field.shape[:2]
    even = lax.rem(lax.axis_index("gx"), 2) == 0
    near_at = jnp.where(even, bx - 1, 0)
    far_at = jnp.where(even, 0, bx - 1)

    @pl.loop(0, by)
    def _(y):
        near[y] = field[near_at, y]
        far[y] = field[far_at, y]

    @pl.loop(0, bx)
    def _(x):
        low_y[x] = field[x, 0]
        high_y[x] = field[x, by - 1]


def first_kernel(drift, value, field, row, near, far, low_y, high_y, rate_out, table, wind, raw, sems):
    bx, by = field.shape[:2]
    copies = [pltpu.make_async_copy(value.at[x], raw.at[x], sems.at[x]) for x in range(bx)]
    for copy in copies:
        copy.start()
    low = iota(1) < NW
    heading = iota(0)
    cosine = jnp.zeros(TILE, jnp.float32)
    sine = jnp.zeros(TILE, jnp.float32)
    for a in range(NTH):
        angle = np.float32(a) * np.float32(HEAD_STEP)
        cosine = jnp.where(heading == a, np.cos(angle), cosine)
        sine = jnp.where(heading == a, np.sin(angle), sine)
    for j in range(SLABS):
        index = (j + SLABS * (iota(1) // NW)).astype(jnp.float32)
        speed = (SPEED_BASE + index * SPEED_STEP) * (1.0 / SPACE_STEP)
        table[0, :, lanes(j)] = cosine * speed
        table[1, :, lanes(j)] = sine * speed
    for x in range(bx):
        for d in range(2):
            wind[d, x] = jnp.broadcast_to(
                drift[x, :, d : d + 1] * (1.0 / SPACE_STEP), wind.shape[2:]
            )

    moving = jnp.zeros(TILE, jnp.float32)
    for x in range(bx):

        def rate_of(y, peak, x=x):
            east, north = wind_at(wind, x, y)
            for j in range(SLABS):
                peak = jnp.maximum(
                    peak,
                    jnp.abs(table[0, :, lanes(j)] + east) + jnp.abs(table[1, :, lanes(j)] + north),
                )
            return peak

        moving = walk(by, 4, rate_of, moving)
    turn = -1.0 + ((iota(1) % NW).astype(jnp.float32) + 0.5) * (2.0 / NW)
    turn_top = jnp.max(jnp.abs(turn), keepdims=True) / HEAD_STEP
    rate = jnp.max(moving, keepdims=True) + turn_top + TURN_LIMIT / TURN_STEP
    rate_row = jnp.broadcast_to(rate, (1, LANES))
    rate_out[...] = rate_row

    peak = jnp.zeros(TILE, jnp.float32)
    for x in range(bx):
        copies[x].wait()

        def gap_of(y, peak, x=x):
            cells = apart(load(raw, x, y), low)
            store(field, cells, x, y)
            return speed_gap(peak, cells, low)

        peak = walk(by, 2, gap_of, peak)
    row[...] = gap_row(peak, rate_row, low)
    fill_edges(field, near, far, low_y, high_y)


def slope_kernel(first, table, wind, near, far, from_low, from_high, center, limit, *refs):
    parts, refs = refs[:5], refs[5:]
    if first:
        barrier, kept, field, raw, sem = refs
        fetch = pltpu.make_async_copy(limit, raw, sem)
    else:
        barrier, field, sem = refs
        fetch = pltpu.make_async_copy(limit, barrier, sem)
    fetch.start()
    bx, by = center.shape[:2]
    gx, gy = lax.axis_index("gx"), lax.axis_index("gy")
    even = lax.rem(gx, 2) == 0
    near_at = jnp.where(even, bx + 1, 0)
    far_at = jnp.where(even, 0, bx + 1)

    @pl.loop(0, by)
    def _(y):
        field[near_at, y + 1] = near[y]
        field[far_at, y + 1] = far[y]
        for x in range(bx):
            field[x + 1, y + 1] = center[x, y]

    @pl.loop(0, bx)
    def _(x):
        field[x + 1, 0] = from_low[x]
        field[x + 1, by + 1] = from_high[x]

    def extend(edge, along_x, at, end, inner):
        @pl.when(edge)
        def _():
            @pl.loop(0, by if along_x else bx)
            def _(i):
                if along_x:
                    field[at, i + 1] = 2.0 * field[end, i + 1] - field[inner, i + 1]
                else:
                    field[i + 1, at] = 2.0 * field[i + 1, end] - field[i + 1, inner]

    extend(gx == 0, True, 0, 1, 2)
    extend(gx == lax.axis_size("gx") - 1, True, bx + 1, bx, bx - 1)
    extend(gy == 0, False, 0, 1, 2)
    extend(gy == lax.axis_size("gy") - 1, False, by + 1, by, by - 1)

    lane = iota(1)
    low = lane < NW
    turn = -1.0 + ((lane % NW).astype(jnp.float32) + 0.5) * (2.0 / NW)
    turn_up = turn > 0.0
    turn_rate = jnp.abs(turn) / HEAD_STEP
    turn_first = lane % NW == 0
    turn_last = lane % NW == NW - 1

    for part, start, x, y_start, length in runs(bx, by):

        def slopes(i, carry, part=part, start=start, x=x, y_start=y_start):
            y = y_start + i
            east_wind, north_wind = wind_at(wind, x, y)
            cells = load(field, x + 1, y + 1)
            for j in range(SLABS):
                c = cells[j]
                twice = c + c
                east = table[0, :, lanes(j)] + east_wind
                ahead = jnp.where(
                    east > 0.0, field[x + 2, y + 1, :, lanes(j)], field[x, y + 1, :, lanes(j)]
                )
                total = jnp.abs(east) * (ahead - c)
                north = table[1, :, lanes(j)] + north_wind
                ahead = jnp.where(
                    north > 0.0, field[x + 1, y + 2, :, lanes(j)], field[x + 1, y, :, lanes(j)]
                )
                total += jnp.abs(north) * (ahead - c)
                ahead = jnp.where(
                    turn_up, pltpu.roll(c, NTH - 1, axis=0), pltpu.roll(c, 1, axis=0)
                )
                total += turn_rate * (ahead - c)
                after = pltpu.roll(c, LANES - 1, axis=1)
                before = pltpu.roll(c, 1, axis=1)
                ahead = jnp.maximum(
                    jnp.where(turn_last, twice - before, after),
                    jnp.where(turn_first, twice - after, before),
                )
                total += (TURN_LIMIT / TURN_STEP) * (ahead - c)
                after, before = speed_sides(cells, j, low, twice)
                change = after - before
                total += (change * change) * (
                    0.25 / (SPEED_STEP * SPEED_STEP) / (2.0 * EFFORT_COST)
                )
                parts[part][start + i, :, lanes(j)] = total
            return carry

        walk(length, 2, slopes, 0)

    fetch.wait()
    if first:
        for x in range(bx):

            def rearrange(y, carry, x=x):
                store(barrier, apart(load(raw, x, y), low), x, y)
                return carry

            walk(by, 2, rearrange, 0)
        keep = pltpu.make_async_copy(barrier, kept, sem)
        keep.start()
        keep.wait()


def update_kernel(step, last, got, barrier, rate_row, steps_in, field_in, *refs):
    parts, refs = refs[:5], refs[5:]
    bx, by = field_in.shape[:2]
    lane = lax.broadcasted_iota(jnp.int32, (1, LANES), 1)
    both = jnp.max(got[...], axis=0)
    gap = jnp.max(jnp.where(lane < NW, both, 0.0), keepdims=True)
    rate = jnp.max(jnp.where(lane < NW, 0.0, both), keepdims=True)
    top_slope = gap / SPEED_STEP
    time_step = COURANT / (rate + top_slope / (EFFORT_COST * SPEED_STEP))
    weight = jnp.broadcast_to(time_step, TILE)
    weight_scaled = jnp.broadcast_to(
        time_step * (top_slope / EFFORT_COST) * (0.5 / SPEED_STEP), TILE
    )
    steps = jnp.where(lane == step, time_step, steps_in[...])
    low = iota(1) < NW
    if last:
        value_out, steps_out, field_out, sems = refs
        for i in range(ITERS):
            steps_out[i] = steps[0, i]
    else:
        field_out, near, far, low_y, high_y, row, steps_out = refs
        steps_out[...] = steps

    copies = []
    peak = jnp.zeros(TILE, jnp.float32)
    for part, start, x, y_start, length in runs(bx, by):

        def update(i, peak, part=part, start=start, x=x, y_start=y_start):
            y = y_start + i
            old = load(field_in, x, y)
            cells = []
            for j in range(SLABS):
                twice = old[j] + old[j]
                after, before = speed_sides(old, j, low, twice)
                value = old[j] + weight * parts[part][start + i, :, lanes(j)]
                value += weight_scaled * ((after + before) - twice)
                cells.append(jnp.minimum(value, barrier[x, y, :, lanes(j)]))
            if last:
                store(field_out, together(cells, low), x, y)
                return peak
            store(field_out, cells, x, y)
            return speed_gap(peak, cells, low)

        peak = walk(length, 4, update, peak)
        if last and y_start + length == by:
            copies.append(pltpu.make_async_copy(field_out.at[x], value_out.at[x], sems.at[x]))
            copies[-1].start()
    for copy in copies:
        copy.wait()
    if not last:
        row[...] = gap_row(peak, rate_row[...], low)
        fill_edges(field_out, near, far, low_y, high_y)


def hold(*arrays, space=pltpu.VMEM):
    return [pltpu.with_memory_space_constraint(a, space) for a in arrays]


def swap(cells, axis, first):
    count = lax.axis_size(axis)
    pairs = [(i, (i + 1) % count) for i in range(first, count, 2)]
    return lax.ppermute(cells, axis, pairs + [(j, i) for i, j in pairs])


def shift(cells, axis, way):
    count = lax.axis_size(axis)
    return lax.ppermute(cells, axis, [(i, (i + way) % count) for i in range(count)])


def per_device(value_field, obstacle, drift_field):
    bx, by = value_field.shape[:2]
    cells = value_field.shape[2:]
    size = value_field.size
    devices = lax.axis_size("gx") * lax.axis_size("gy")

    def in_vmem(*shape):
        return pltpu.VMEM(shape, jnp.float32)

    block = in_vmem(bx, by, *cells)
    parts = [in_vmem(n, *cells) for n in part_sizes(bx, by)]
    edges = parts[:4]
    row = in_vmem(1, LANES)
    in_hbm = jax.ShapeDtypeStruct(value_field.shape, jnp.float32)
    vmem, smem, hbm = (pl.BlockSpec(memory_space=m) for m in (pltpu.VMEM, pltpu.SMEM, pltpu.HBM))

    def call(kernel, outs, *, out_specs=None, ins, in_specs=None, scratch=(), aliases={}):
        return pl.pallas_call(
            kernel,
            out_shape=tuple(outs),
            in_specs=in_specs or [vmem] * len(ins),
            out_specs=out_specs or [vmem] * len(outs),
            scratch_shapes=scratch,
            input_output_aliases=aliases,
            compiler_params=pltpu.CompilerParams(vmem_limit_bytes=VMEM_LIMIT),
            cost_estimate=pl.CostEstimate(
                flops=40 * size, bytes_accessed=16 * size, transcendentals=0
            ),
        )(*ins)

    outs = [block, row, *edges, row, in_vmem(2, *cells), in_vmem(2, bx, by, LANES)]
    field, sent, near, far, low_y, high_y, rate_row, table, wind = call(
        first_kernel,
        outs,
        ins=[drift_field, *hold(value_field, space=pltpu.HBM)],
        in_specs=[vmem, hbm],
        scratch=[pltpu.VMEM(value_field.shape, jnp.float32), pltpu.SemaphoreType.DMA((bx,))],
    )
    steps = jnp.zeros((1, LANES), jnp.float32)
    (limit,) = hold(obstacle, space=pltpu.HBM)
    padded = pltpu.VMEM((bx + 2, by + 2, *cells), jnp.float32)

    for step in range(ITERS):
        first, last = step == 0, step == ITERS - 1
        got_edges = [
            swap(near, "gx", 0),
            swap(far, "gx", 1),
            shift(high_y, "gy", 1),
            shift(low_y, "gy", -1),
        ]
        rows = jnp.broadcast_to(sent[None], (devices, 1, LANES))
        got = lax.all_to_all(rows, ("gx", "gy"), 0, 0)
        outs = [*parts, block] + [pltpu.HBM(value_field.shape, jnp.float32)] * first
        ins = [*hold(table, wind, *got_edges, field), limit]
        result = call(
            functools.partial(slope_kernel, first),
            outs,
            out_specs=[vmem] * 6 + [hbm] * first,
            ins=ins,
            in_specs=[vmem] * 7 + [hbm],
            scratch=[padded]
            + [pltpu.VMEM(value_field.shape, jnp.float32)] * first
            + [pltpu.SemaphoreType.DMA],
            aliases={2 + i: i for i in range(4)},
        )
        slopes, barrier = result[:5], result[5]
        if first:
            (limit,) = hold(result[6], space=pltpu.HBM)
        ins = hold(got, barrier, rate_row, steps, field, *slopes)
        if last:
            return call(
                functools.partial(update_kernel, step, True),
                [in_hbm, jax.ShapeDtypeStruct((ITERS,), jnp.float32)],
                out_specs=[hbm, smem],
                ins=ins,
                scratch=[
                    pltpu.VMEM(value_field.shape, jnp.float32),
                    pltpu.SemaphoreType.DMA((bx,)),
                ],
            )
        field, near, far, low_y, high_y, sent, steps = call(
            functools.partial(update_kernel, step, False),
            [block, *edges, row, row],
            ins=ins,
            aliases={4: 0, **{5 + i: 1 + i for i in range(4)}},
        )


def solution(mesh):
    return jax.shard_map(
        per_device,
        mesh=mesh,
        in_specs=(P("gx", "gy", None, None), P("gx", "gy", None, None), P("gx", "gy", None)),
        out_specs=(P("gx", "gy", None, None), P()),
        check_vma=False,
    )
```

time: 266 us -> 80.9 us (0.30)
  blocking collectives: 178 us -> 0 us
  Pallas kernels: 0 us -> 28.3 us
  other arithmetic: 22.4 us -> 0 us
  between operations: 9.32 us -> 0.75 us
  waiting for transfers between devices: 20.1 us -> 16.8 us
    pmax x4 -> x0, blocking collectives: 178 us -> none  [the longest x3 136 us: per_device(): slope_peak = lax.pmax(local_slope, ('gx', 'gy'))]
    pallas_call x0 -> x9, Pallas kernels: none -> 28.3 us  [call(): pl.pallas_call(kernel, out_shape=tuple(outs), in_specs=in_specs or [vmem]...]
    ppermute x16, waiting for transfers between devices: 20.1 us -> 6.74 us  [the longest x8 6.37 us: shift(): lax.ppermute(cells, axis, [(i, (i + way) % count) for i in range(count)])]
    min x4 -> x0, other arithmetic: 11.8 us -> none  [advance(): return jnp.minimum(center + time_step * (hamiltonian + damping), barrier)]
    all_to_all x0 -> x4, starting transfers between devices: none -> 10.1 us  [per_device(): got = lax.all_to_all(rows, ('gx', 'gy'), 0, 0)]
    all_to_all x0 -> x4, waiting for transfers between devices: none -> 10 us  [per_device(): got = lax.all_to_all(rows, ('gx', 'gy'), 0, 0)]
    ppermute x16, starting transfers between devices: 29.1 us -> 21.5 us  [the longest x8 15.3 us: shift(): lax.ppermute(cells, axis, [(i, (i + way) % count) for i in range(count)])]
    reduce_max x5 -> x0, other arithmetic: 4.83 us -> none  [the longest x4 3.86 us: per_device(): jnp.max(jnp.abs(current_value[..., NW:] - current_value[..., :-NW]))]
  transfers between devices with their start and end apart: 16 -> 20, of which waited for: 5 -> 13; matrix products, arithmetic and copies ran while one was open for 2% -> 3% of each run, Pallas kernels for 0% -> 15%
where the time goes in v1:
time: 80.9 us; the launch traced here: 80.6 us
  starting transfers between devices  31.6 us (39%)
  Pallas kernels  28.3 us (35%)
  waiting for transfers between devices  16.8 us (21%)
  local copies, waits for them, and re-layouts  3.2 us (4%)
    pallas_call x9, Pallas kernels, call(): pl.pallas_call(kernel, out_shape=tuple(outs), in_specs=in_specs or [vmem]...  28.3 us
    ppermute x8, starting transfers between devices, shift(): lax.ppermute(cells, axis, [(i, (i + way) % count) for i in range(count)])  15.3 us
    all_to_all x4, starting transfers between devices, per_device(): got = lax.all_to_all(rows, ('gx', 'gy'), 0, 0)  10.1 us
    all_to_all x4, waiting for transfers between devices, per_device(): got = lax.all_to_all(rows, ('gx', 'gy'), 0, 0)  10 us
    ppermute x8, waiting for transfers between devices, shift(): lax.ppermute(cells, axis, [(i, (i + way) % count) for i in range(count)])  6.37 us
    ppermute x8, starting transfers between devices, swap(): return lax.ppermute(cells, axis, pairs + [(j, i) for i, j in pairs])  6.19 us
    broadcast_in_dim x4, local copies, waits for them, and re-layouts, per_device(): rows = jnp.broadcast_to(sent[None], (devices, 1, LANES))  2.42 us
  transfers between devices with their start and end apart: 20, of which 13 were waited for; matrix products, arithmetic and copies ran while one was open for 3% of the time, Pallas kernels for 15%

profile of v1, /device:TPU:0, one launch (start us, length us, event | category | flops | bytes accessed | tf_op | source)
XLA Modules:
  0.0 80.6 jit_solution(169657663522109825)
XLA Ops:
  0.6 0.8 copy.36.drift
  1.4 3.6 %shard_map.50 = (f32[4,8,8,1024]{3,2,1,0:T(8,128)S(1)}, f32[1,128]{1,0:T(1,128)S(1)}, f32[8,8,1024]{2,1,0:T(8,128)S(1)}, f32[8,8,1024]{2,1,0:T(8,128)S(1)}, f32[...) custom-call(f32[4,8,2]{2,1,0:T(8,128)S(1)} %copy.36.drift, ...), custom_call_target="tpu_custom_call" | custom-call | flops 10485760 | bytes 4194304 | tf_op jit(solution)/shard_map/pallas_call | solution.py:387
  5.6 3.5 %collective-permute-start.1 = (f32[8,8,1024]{2,1,0:T(8,128)S(1)}, f32[8,8,1024]{2,1,0:T(8,128)S(1)}, u32[]{:S(2)}, u32[]{:S(2)}) collective-permute-start(f32[8,8,1024]{2,1,0:T(8,128)S(1)} %get-tuple-element.61), channel_id=1, source_target_pairs={{4,8},{12,16},{20,24},{28,0},{8,4},{16,12},{24,20},{0,28},{5,9},{1... | collective-permute-start | bytes 786440 | tf_op jit(solution)/shard_map/ppermute | solution.py:362
  9.1 1.6 %collective-permute-start.2 = (f32[4,8,1024]{2,1,0:T(8,128)S(1)}, f32[4,8,1024]{2,1,0:T(8,128)S(1)}, u32[]{:S(2)}, u32[]{:S(2)}) collective-permute-start(f32[4,8,1024]{2,1,0:T(8,128)S(1)} %get-tuple-element.62), channel_id=1, source_target_pairs={{0,1},{1,2},{2,3},{3,0},{4,5},{5,6},{6,7},{7,4},{8,9},{9,10},{10,1... | collective-permute-start | bytes 393224 | tf_op jit(solution)/shard_map/ppermute | solution.py:367
  10.7 2.2 %collective-permute-start.3 = (f32[4,8,1024]{2,1,0:T(8,128)S(1)}, f32[4,8,1024]{2,1,0:T(8,128)S(1)}, u32[]{:S(2)}, u32[]{:S(2)}) collective-permute-start(f32[4,8,1024]{2,1,0:T(8,128)S(1)} %get-tuple-element.63), channel_id=1, source_target_pairs={{0,3},{1,0},{2,1},{3,2},{4,7},{5,4},{6,5},{7,6},{8,11},{9,8},{10,9... | collective-permute-start | bytes 393224 | tf_op jit(solution)/shard_map/ppermute | solution.py:367
  13.5 2.6 %all-to-all-start = ((f32[32,1,128]{2,1,0:T(1,128)}), f32[32,1,128]{2,1,0:T(1,128)S(1)}, u32[]{:S(2)}, u32[]{:S(2)}) async-start(f32[32,1,128]{2,1,0:T(1,128)} %broadcast_in_dim.36), calls=%async_computation | async-start | bytes 32768 | tf_op jit(solution)/shard_map/all_to_all | solution.py:421
  16.1 0.8 %collective-permute-done.2.from_low = f32[4,8,1024]{2,1,0:T(8,128)S(1)} collective-permute-done((f32[4,8,1024]{2,1,0:T(8,128)S(1)}, f32[4,8,1024]{2,1,0:T(8,128)S(1)}, u32[]{:S(2)}, u32[]{:S(2)}) %collective-permute-start.2) | collective-permute-done | bytes 131104 | tf_op jit(solution)/shard_map/ppermute | solution.py:367
  17.0 0.8 collective-permute-done.3.from_high
  17.7 4.4 %shard_map.51 = (f32[8,8,1024]{2,1,0:T(8,128)S(1)}, f32[8,8,1024]{2,1,0:T(8,128)S(1)}, f32[4,8,1024]{2,1,0:T(8,128)S(1)}, f32[4,8,1024]{2,1,0:T(8,128)S(1)}, f32...) custom-call(f32[2,8,1024]{2,1,0:T(8,128)S(1)} %get-tuple-element.58., ...), custom_call_target="tpu_custom_call", output_to_operand_aliasing={{0}: (2, {}), {1}: (3, {}), {2}: (4, {}), {3}: (5, {})} | custom-call | flops 10485760 | bytes 4194304 | tf_op jit(solution)/shard_map/pallas_call | solution.py:387
  22.1 1.2 %all-to-all-done.got = f32[32,1,128]{2,1,0:T(1,128)S(1)} async-done(((f32[32,1,128]{2,1,0:T(1,128)}), f32[32,1,128]{2,1,0:T(1,128)S(1)}, u32[]{:S(2)}, u32[]{:S(2)}) %all-to-all-start) | async-done | bytes 16416 | tf_op jit(solution)/shard_map/all_to_all | solution.py:421
  23.3 2.9 %shard_map.52 = (f32[4,8,8,1024]{3,2,1,0:T(8,128)S(1)}, f32[8,8,1024]{2,1,0:T(8,128)S(1)}, f32[8,8,1024]{2,1,0:T(8,128)S(1)}, f32[4,8,1024]{2,1,0:T(8,128)S(1)},...) custom-call(f32[32,1,128]{2,1,0:T(1,128)S(1)} %all-to-all-done.got, ...), custom_call_target="tpu_custom_call", output_to_operand_aliasing={{0}: (4, {}), {1}: (5, {}), {2}: (6, {}), {3}: (7, {}), {4}... | custom-call | flops 10485760 | bytes 4194304 | tf_op jit(solution)/shard_map/pallas_call | solution.py:387
  26.2 0.6 collective-permute-start.5
  26.9 0.8 collective-permute-start.6
  27.7 3.1 %collective-permute-start.7 = (f32[4,8,1024]{2,1,0:T(8,128)S(1)}, f32[4,8,1024]{2,1,0:T(8,128)}, u32[]{:S(2)}, u32[]{:S(2)}) collective-permute-start(f32[4,8,1024]{2,1,0:T(8,128)S(1)} %get-tuple-element.76), channel_id=1, source_target_pairs={{0,3},{1,0},{2,1},{3,2},{4,7},{5,4},{6,5},{7,6},{8,11},{9,8},{10,9... | collective-permute-start | bytes 393224 | tf_op jit(solution)/shard_map/ppermute | solution.py:367
  31.3 2.5 %all-to-all-start.1 = ((f32[32,1,128]{2,1,0:T(1,128)}), f32[32,1,128]{2,1,0:T(1,128)S(1)}, u32[]{:S(2)}, u32[]{:S(2)}) async-start(f32[32,1,128]{2,1,0:T(1,128)} %broadcast_in_dim.39), calls=%async_computation.1 | async-start | bytes 32768 | tf_op jit(solution)/shard_map/all_to_all | solution.py:421
  33.8 1.3 %collective-permute-done.6.from_low = f32[4,8,1024]{2,1,0:T(8,128)S(1)} collective-permute-done((f32[4,8,1024]{2,1,0:T(8,128)S(1)}, f32[4,8,1024]{2,1,0:T(8,128)S(1)}, u32[]{:S(2)}, u32[]{:S(2)}) %collective-permute-start.6) | collective-permute-done | bytes 131104 | tf_op jit(solution)/shard_map/ppermute | solution.py:367
  35.6 3.6 %shard_map.53 = (f32[8,8,1024]{2,1,0:T(8,128)S(1)}, f32[8,8,1024]{2,1,0:T(8,128)S(1)}, f32[4,8,1024]{2,1,0:T(8,128)S(1)}, f32[4,8,1024]{2,1,0:T(8,128)}, f32[8,8...) custom-call(f32[2,8,1024]{2,1,0:T(8,128)S(1)} %get-tuple-element.58., ...), custom_call_target="tpu_custom_call", output_to_operand_aliasing={{0}: (2, {}), {1}: (3, {}), {2}: (4, {}), {3}: (5, {})} | custom-call | flops 10485760 | bytes 4194304 | tf_op jit(solution)/shard_map/pallas_call | solution.py:387
  39.1 1.9 %all-to-all-done.1.got = f32[32,1,128]{2,1,0:T(1,128)S(1)} async-done(((f32[32,1,128]{2,1,0:T(1,128)}), f32[32,1,128]{2,1,0:T(1,128)S(1)}, u32[]{:S(2)}, u32[]{:S(2)}) %all-to-all-start.1) | async-done | bytes 16416 | tf_op jit(solution)/shard_map/all_to_all | solution.py:421
  41.0 4.4 %shard_map.54 = (f32[4,8,8,1024]{3,2,1,0:T(8,128)S(1)}, f32[8,8,1024]{2,1,0:T(8,128)S(1)}, f32[8,8,1024]{2,1,0:T(8,128)S(1)}, f32[4,8,1024]{2,1,0:T(8,128)S(1)},...) custom-call(f32[32,1,128]{2,1,0:T(1,128)S(1)} %all-to-all-done.1.got, ...), custom_call_target="tpu_custom_call", output_to_operand_aliasing={{0}: (4, {}), {1}: (5, {}), {2}: (6, {}), {3}: (7, {}), {4}... | custom-call | flops 10485760 | bytes 4194304 | tf_op jit(solution)/shard_map/pallas_call | solution.py:387
  45.4 0.7 collective-permute-start.9
  46.6 3.3 %collective-permute-start.11 = (f32[4,8,1024]{2,1,0:T(8,128)S(1)}, f32[4,8,1024]{2,1,0:T(8,128)S(1)}, u32[]{:S(2)}, u32[]{:S(2)}) collective-permute-start(f32[4,8,1024]{2,1,0:T(8,128)S(1)} %get-tuple-element.90), channel_id=1, source_target_pairs={{0,3},{1,0},{2,1},{3,2},{4,7},{5,4},{6,5},{7,6},{8,11},{9,8},{10,9... | collective-permute-start | bytes 393224 | tf_op jit(solution)/shard_map/ppermute | solution.py:367
  50.5 2.5 %all-to-all-start.2 = ((f32[32,1,128]{2,1,0:T(1,128)}), f32[32,1,128]{2,1,0:T(1,128)S(1)}, u32[]{:S(2)}, u32[]{:S(2)}) async-start(f32[32,1,128]{2,1,0:T(1,128)} %broadcast_in_dim.41), calls=%async_computation.2 | async-start | bytes 32768 | tf_op jit(solution)/shard_map/all_to_all | solution.py:421
  53.0 1.5 %collective-permute-done.10.from_low = f32[4,8,1024]{2,1,0:T(8,128)S(1)} collective-permute-done((f32[4,8,1024]{2,1,0:T(8,128)}, f32[4,8,1024]{2,1,0:T(8,128)S(1)}, u32[]{:S(2)}, u32[]{:S(2)}) %collective-permute-start.10) | collective-permute-done | bytes 131104 | tf_op jit(solution)/shard_map/ppermute | solution.py:367
  54.8 2.0 %shard_map.55 = (f32[8,8,1024]{2,1,0:T(8,128)S(1)}, f32[8,8,1024]{2,1,0:T(8,128)S(1)}, f32[4,8,1024]{2,1,0:T(8,128)S(1)}, f32[4,8,1024]{2,1,0:T(8,128)S(1)}, f32...) custom-call(f32[2,8,1024]{2,1,0:T(8,128)S(1)} %get-tuple-element.58., ...), custom_call_target="tpu_custom_call", output_to_operand_aliasing={{0}: (2, {}), {1}: (3, {}), {2}: (4, {}), {3}: (5, {})} | custom-call | flops 10485760 | bytes 4194304 | tf_op jit(solution)/shard_map/pallas_call | solution.py:387
  56.8 3.4 %all-to-all-done.2.got = f32[32,1,128]{2,1,0:T(1,128)S(1)} async-done(((f32[32,1,128]{2,1,0:T(1,128)}), f32[32,1,128]{2,1,0:T(1,128)S(1)}, u32[]{:S(2)}, u32[]{:S(2)}) %all-to-all-start.2) | async-done | bytes 16416 | tf_op jit(solution)/shard_map/all_to_all | solution.py:421
  60.2 2.9 %shard_map.56 = (f32[4,8,8,1024]{3,2,1,0:T(8,128)S(1)}, f32[8,8,1024]{2,1,0:T(8,128)S(1)}, f32[8,8,1024]{2,1,0:T(8,128)S(1)}, f32[4,8,1024]{2,1,0:T(8,128)S(1)},...) custom-call(f32[32,1,128]{2,1,0:T(1,128)S(1)} %all-to-all-done.2.got, ...), custom_call_target="tpu_custom_call", output_to_operand_aliasing={{0}: (4, {}), {1}: (5, {}), {2}: (6, {}), {3}: (7, {}), {4}... | custom-call | flops 10485760 | bytes 4194304 | tf_op jit(solution)/shard_map/pallas_call | solution.py:387
  64.4 3.3 %collective-permute-start.15 = (f32[4,8,1024]{2,1,0:T(8,128)S(1)}, f32[4,8,1024]{2,1,0:T(8,128)S(1)}, u32[]{:S(2)}, u32[]{:S(2)}) collective-permute-start(f32[4,8,1024]{2,1,0:T(8,128)S(1)} %get-tuple-element.103), channel_id=1, source_target_pairs={{0,3},{1,0},{2,1},{3,2},{4,7},{5,4},{6,5},{7,6},{8,11},{9,8},{10,9... | collective-permute-start | bytes 393224 | tf_op jit(solution)/shard_map/ppermute | solution.py:367
  68.3 2.6 %all-to-all-start.3 = ((f32[32,1,128]{2,1,0:T(1,128)}), f32[32,1,128]{2,1,0:T(1,128)S(1)}, u32[]{:S(2)}, u32[]{:S(2)}) async-start(f32[32,1,128]{2,1,0:T(1,128)} %broadcast_in_dim.43), calls=%async_computation.3 | async-start | bytes 32768 | tf_op jit(solution)/shard_map/all_to_all | solution.py:421
  70.8 1.2 %collective-permute-done.14.from_low = f32[4,8,1024]{2,1,0:T(8,128)S(1)} collective-permute-done((f32[4,8,1024]{2,1,0:T(8,128)S(1)}, f32[4,8,1024]{2,1,0:T(8,128)S(1)}, u32[]{:S(2)}, u32[]{:S(2)}) %collective-permute-start.14) | collective-permute-done | bytes 131104 | tf_op jit(solution)/shard_map/ppermute | solution.py:367
  72.5 2.0 %shard_map.57 = (f32[8,8,1024]{2,1,0:T(8,128)S(1)}, f32[8,8,1024]{2,1,0:T(8,128)S(1)}, f32[4,8,1024]{2,1,0:T(8,128)S(1)}, f32[4,8,1024]{2,1,0:T(8,128)S(1)}, f32...) custom-call(f32[2,8,1024]{2,1,0:T(8,128)S(1)} %get-tuple-element.58., ...), custom_call_target="tpu_custom_call", output_to_operand_aliasing={{0}: (2, {}), {1}: (3, {}), {2}: (4, {}), {3}: (5, {})} | custom-call | flops 10485760 | bytes 4194304 | tf_op jit(solution)/shard_map/pallas_call | solution.py:387
  74.5 3.5 %all-to-all-done.3.got = f32[32,1,128]{2,1,0:T(1,128)S(1)} async-done(((f32[32,1,128]{2,1,0:T(1,128)}), f32[32,1,128]{2,1,0:T(1,128)S(1)}, u32[]{:S(2)}, u32[]{:S(2)}) %all-to-all-start.3) | async-done | bytes 16416 | tf_op jit(solution)/shard_map/all_to_all | solution.py:421
  78.0 2.6 %shard_map.58 = (f32[4,8,8,1024]{3,2,1,0:T(8,128)}, f32[4]{0:T(128)}) custom-call(f32[32,1,128]{2,1,0:T(1,128)S(1)} %all-to-all-done.3.got, f32[4,8,8,1024]{3,2,1,0:T(8,128)S(1)} %get-tuple-element.105.barrier, f32[1,128]{1,0:T(1,128)S(1)} %get-tuple-element.66.rate_row, f32[1,128]{1,0:T(1,128)S(1)} %get-tuple-element.106.steps_in, ...), custom_call_target="tpu_custom_call" | custom-call | flops 10485760 | bytes 4194304 | tf_op jit(solution)/shard_map/pallas_call | solution.py:387
  (23 shorter events, 6.0 us)
Async XLA Ops:
  5.0 12.7 %collective-permute-start = (f32[8,8,1024]{2,1,0:T(8,128)S(1)}, f32[8,8,1024]{2,1,0:T(8,128)S(1)}, u32[]{:S(2)}, u32[]{:S(2)}) collective-permute-start(f32[8,8,1024]{2,1,0:T(8,128)S(1)} %get-tuple-element.60), channel_id=1, source_target_pairs={{0,4},{8,12},{16,20},{24,28},{4,0},{12,8},{20,16},{28,24},{1,5},{9... | collective-permute-start | bytes 786440 | tf_op jit(solution)/shard_map/ppermute | solution.py:362
  5.6 12.2 %collective-permute-start.1 = (f32[8,8,1024]{2,1,0:T(8,128)S(1)}, f32[8,8,1024]{2,1,0:T(8,128)S(1)}, u32[]{:S(2)}, u32[]{:S(2)}) collective-permute-start(f32[8,8,1024]{2,1,0:T(8,128)S(1)} %get-tuple-element.61), channel_id=1, source_target_pairs={{4,8},{12,16},{20,24},{28,0},{8,4},{16,12},{24,20},{0,28},{5,9},{1... | collective-permute-start | bytes 786440 | tf_op jit(solution)/shard_map/ppermute | solution.py:362
  9.1 7.9 %collective-permute-start.2 = (f32[4,8,1024]{2,1,0:T(8,128)S(1)}, f32[4,8,1024]{2,1,0:T(8,128)S(1)}, u32[]{:S(2)}, u32[]{:S(2)}) collective-permute-start(f32[4,8,1024]{2,1,0:T(8,128)S(1)} %get-tuple-element.62), channel_id=1, source_target_pairs={{0,1},{1,2},{2,3},{3,0},{4,5},{5,6},{6,7},{7,4},{8,9},{9,10},{10,1... | collective-permute-start | bytes 393224 | tf_op jit(solution)/shard_map/ppermute | solution.py:367
  10.7 7.1 %collective-permute-start.3 = (f32[4,8,1024]{2,1,0:T(8,128)S(1)}, f32[4,8,1024]{2,1,0:T(8,128)S(1)}, u32[]{:S(2)}, u32[]{:S(2)}) collective-permute-start(f32[4,8,1024]{2,1,0:T(8,128)S(1)} %get-tuple-element.63), channel_id=1, source_target_pairs={{0,3},{1,0},{2,1},{3,2},{4,7},{5,4},{6,5},{7,6},{8,11},{9,8},{10,9... | collective-permute-start | bytes 393224 | tf_op jit(solution)/shard_map/ppermute | solution.py:367
  13.5 9.8 %all-to-all-start = ((f32[32,1,128]{2,1,0:T(1,128)}), f32[32,1,128]{2,1,0:T(1,128)S(1)}, u32[]{:S(2)}, u32[]{:S(2)}) async-start(f32[32,1,128]{2,1,0:T(1,128)} %broadcast_in_dim.36), calls=%async_computation | async-start | bytes 32768 | tf_op jit(solution)/shard_map/all_to_all | solution.py:421
  26.2 9.4 %collective-permute-start.4 = (f32[8,8,1024]{2,1,0:T(8,128)S(1)}, f32[8,8,1024]{2,1,0:T(8,128)S(1)}, u32[]{:S(2)}, u32[]{:S(2)}) collective-permute-start(f32[8,8,1024]{2,1,0:T(8,128)S(1)} %get-tuple-element.73), channel_id=1, source_target_pairs={{0,4},{8,12},{16,20},{24,28},{4,0},{12,8},{20,16},{28,24},{1,5},{9... | collective-permute-start | bytes 786440 | tf_op jit(solution)/shard_map/ppermute | solution.py:362
  26.2 9.3 %collective-permute-start.5 = (f32[8,8,1024]{2,1,0:T(8,128)S(1)}, f32[8,8,1024]{2,1,0:T(8,128)S(1)}, u32[]{:S(2)}, u32[]{:S(2)}) collective-permute-start(f32[8,8,1024]{2,1,0:T(8,128)S(1)} %get-tuple-element.74), channel_id=1, source_target_pairs={{4,8},{12,16},{20,24},{28,0},{8,4},{16,12},{24,20},{0,28},{5,9},{1... | collective-permute-start | bytes 786440 | tf_op jit(solution)/shard_map/ppermute | solution.py:362
  26.9 8.2 %collective-permute-start.6 = (f32[4,8,1024]{2,1,0:T(8,128)S(1)}, f32[4,8,1024]{2,1,0:T(8,128)S(1)}, u32[]{:S(2)}, u32[]{:S(2)}) collective-permute-start(f32[4,8,1024]{2,1,0:T(8,128)S(1)} %get-tuple-element.75), channel_id=1, source_target_pairs={{0,1},{1,2},{2,3},{3,0},{4,5},{5,6},{6,7},{7,4},{8,9},{9,10},{10,1... | collective-permute-start | bytes 393224 | tf_op jit(solution)/shard_map/ppermute | solution.py:367
  27.7 7.9 %collective-permute-start.7 = (f32[4,8,1024]{2,1,0:T(8,128)S(1)}, f32[4,8,1024]{2,1,0:T(8,128)}, u32[]{:S(2)}, u32[]{:S(2)}) collective-permute-start(f32[4,8,1024]{2,1,0:T(8,128)S(1)} %get-tuple-element.76), channel_id=1, source_target_pairs={{0,3},{1,0},{2,1},{3,2},{4,7},{5,4},{6,5},{7,6},{8,11},{9,8},{10,9... | collective-permute-start | bytes 393224 | tf_op jit(solution)/shard_map/ppermute | solution.py:367
  31.3 9.7 %all-to-all-start.1 = ((f32[32,1,128]{2,1,0:T(1,128)}), f32[32,1,128]{2,1,0:T(1,128)S(1)}, u32[]{:S(2)}, u32[]{:S(2)}) async-start(f32[32,1,128]{2,1,0:T(1,128)} %broadcast_in_dim.39), calls=%async_computation.1 | async-start | bytes 32768 | tf_op jit(solution)/shard_map/all_to_all | solution.py:421
  45.4 9.1 %collective-permute-start.8 = (f32[8,8,1024]{2,1,0:T(8,128)S(1)}, f32[8,8,1024]{2,1,0:T(8,128)S(1)}, u32[]{:S(2)}, u32[]{:S(2)}) collective-permute-start(f32[8,8,1024]{2,1,0:T(8,128)S(1)} %get-tuple-element.87), channel_id=1, source_target_pairs={{0,4},{8,12},{16,20},{24,28},{4,0},{12,8},{20,16},{28,24},{1,5},{9... | collective-permute-start | bytes 786440 | tf_op jit(solution)/shard_map/ppermute | solution.py:362
  45.4 9.3 %collective-permute-start.9 = (f32[8,8,1024]{2,1,0:T(8,128)S(1)}, f32[8,8,1024]{2,1,0:T(8,128)S(1)}, u32[]{:S(2)}, u32[]{:S(2)}) collective-permute-start(f32[8,8,1024]{2,1,0:T(8,128)S(1)} %get-tuple-element.88), channel_id=1, source_target_pairs={{4,8},{12,16},{20,24},{28,0},{8,4},{16,12},{24,20},{0,28},{5,9},{1... | collective-permute-start | bytes 786440 | tf_op jit(solution)/shard_map/ppermute | solution.py:362
  46.1 8.4 %collective-permute-start.10 = (f32[4,8,1024]{2,1,0:T(8,128)}, f32[4,8,1024]{2,1,0:T(8,128)S(1)}, u32[]{:S(2)}, u32[]{:S(2)}) collective-permute-start(f32[4,8,1024]{2,1,0:T(8,128)} %get-tuple-element.89), channel_id=1, source_target_pairs={{0,1},{1,2},{2,3},{3,0},{4,5},{5,6},{6,7},{7,4},{8,9},{9,10},{10,1... | collective-permute-start | bytes 393224 | tf_op jit(solution)/shard_map/ppermute | solution.py:367
  46.6 7.9 %collective-permute-start.11 = (f32[4,8,1024]{2,1,0:T(8,128)S(1)}, f32[4,8,1024]{2,1,0:T(8,128)S(1)}, u32[]{:S(2)}, u32[]{:S(2)}) collective-permute-start(f32[4,8,1024]{2,1,0:T(8,128)S(1)} %get-tuple-element.90), channel_id=1, source_target_pairs={{0,3},{1,0},{2,1},{3,2},{4,7},{5,4},{6,5},{7,6},{8,11},{9,8},{10,9... | collective-permute-start | bytes 393224 | tf_op jit(solution)/shard_map/ppermute | solution.py:367
  50.5 9.7 %all-to-all-start.2 = ((f32[32,1,128]{2,1,0:T(1,128)}), f32[32,1,128]{2,1,0:T(1,128)S(1)}, u32[]{:S(2)}, u32[]{:S(2)}) async-start(f32[32,1,128]{2,1,0:T(1,128)} %broadcast_in_dim.41), calls=%async_computation.2 | async-start | bytes 32768 | tf_op jit(solution)/shard_map/all_to_all | solution.py:421
  63.1 9.3 %collective-permute-start.12 = (f32[8,8,1024]{2,1,0:T(8,128)S(1)}, f32[8,8,1024]{2,1,0:T(8,128)S(1)}, u32[]{:S(2)}, u32[]{:S(2)}) collective-permute-start(f32[8,8,1024]{2,1,0:T(8,128)S(1)} %get-tuple-element.100), channel_id=1, source_target_pairs={{0,4},{8,12},{16,20},{24,28},{4,0},{12,8},{20,16},{28,24},{1,5},{9... | collective-permute-start | bytes 786440 | tf_op jit(solution)/shard_map/ppermute | solution.py:362
  63.2 9.3 %collective-permute-start.13 = (f32[8,8,1024]{2,1,0:T(8,128)S(1)}, f32[8,8,1024]{2,1,0:T(8,128)S(1)}, u32[]{:S(2)}, u32[]{:S(2)}) collective-permute-start(f32[8,8,1024]{2,1,0:T(8,128)S(1)} %get-tuple-element.101), channel_id=1, source_target_pairs={{4,8},{12,16},{20,24},{28,0},{8,4},{16,12},{24,20},{0,28},{5,9},{1... | collective-permute-start | bytes 786440 | tf_op jit(solution)/shard_map/ppermute | solution.py:362
  63.8 8.2 %collective-permute-start.14 = (f32[4,8,1024]{2,1,0:T(8,128)S(1)}, f32[4,8,1024]{2,1,0:T(8,128)S(1)}, u32[]{:S(2)}, u32[]{:S(2)}) collective-permute-start(f32[4,8,1024]{2,1,0:T(8,128)S(1)} %get-tuple-element.102), channel_id=1, source_target_pairs={{0,1},{1,2},{2,3},{3,0},{4,5},{5,6},{6,7},{7,4},{8,9},{9,10},{10,1... | collective-permute-start | bytes 393224 | tf_op jit(solution)/shard_map/ppermute | solution.py:367
  64.4 8.0 %collective-permute-start.15 = (f32[4,8,1024]{2,1,0:T(8,128)S(1)}, f32[4,8,1024]{2,1,0:T(8,128)S(1)}, u32[]{:S(2)}, u32[]{:S(2)}) collective-permute-start(f32[4,8,1024]{2,1,0:T(8,128)S(1)} %get-tuple-element.103), channel_id=1, source_target_pairs={{0,3},{1,0},{2,1},{3,2},{4,7},{5,4},{6,5},{7,6},{8,11},{9,8},{10,9... | collective-permute-start | bytes 393224 | tf_op jit(solution)/shard_map/ppermute | solution.py:367
  68.3 9.8 %all-to-all-start.3 = ((f32[32,1,128]{2,1,0:T(1,128)}), f32[32,1,128]{2,1,0:T(1,128)S(1)}, u32[]{:S(2)}, u32[]{:S(2)}) async-start(f32[32,1,128]{2,1,0:T(1,128)} %broadcast_in_dim.43), calls=%async_computation.3 | async-start | bytes 32768 | tf_op jit(solution)/shard_map/all_to_all | solution.py:421

commit v2 on v1

--- a/solution.py
+++ b/solution.py
@@ -85,7 +85,7 @@
 
 
 def wind_at(wind, x, y):
-    return wind[0, x, pl.ds(y, 1), :], wind[1, x, pl.ds(y, 1), :]
+    return wind[0, x, y : y + 1, :], wind[1, x, y : y + 1, :]
 
 
 def gap_row(peak, rate_row, low):
@@ -109,38 +109,28 @@
     return out
 
 
-def walk(length, width, body, carry):
-    width = math.gcd(length, width)
-
-    def trip(t, carry):
-        for i in range(width):
-            carry = body(t * width + i, carry)
-        return carry
-
-    return lax.fori_loop(0, length // width, trip, carry)
-
-
-def fill_edges(field, near, far, low_y, high_y):
+def walk(length, body, carry):
+    for i in range(length):
+        carry = body(i, carry)
+    return carry
+
+
+def fill_edges(field, near_x, far_x, near_y, far_y):
     bx, by = field.shape[:2]
-    even = lax.rem(lax.axis_index("gx"), 2) == 0
-    near_at = jnp.where(even, bx - 1, 0)
-    far_at = jnp.where(even, 0, bx - 1)
-
-    @pl.loop(0, by)
-    def _(y):
-        near[y] = field[near_at, y]
-        far[y] = field[far_at, y]
-
-    @pl.loop(0, bx)
-    def _(x):
-        low_y[x] = field[x, 0]
-        high_y[x] = field[x, by - 1]
-
-
-def first_kernel(drift, value, field, row, near, far, low_y, high_y, rate_out, table, wind, raw, sems):
+    for axis, size, near, far in (("gx", bx, near_x, far_x), ("gy", by, near_y, far_y)):
+        even = lax.rem(lax.axis_index(axis), 2) == 0
+        near_at = jnp.where(even, size - 1, 0)
+        far_at = jnp.where(even, 0, size - 1)
+        for i in range(near.shape[0]):
+            near[i] = field[near_at, i] if axis == "gx" else field[i, near_at]
+            far[i] = field[far_at, i] if axis == "gx" else field[i, far_at]
+
+
+def first_kernel(drift_in, value, field, row, near_x, far_x, near_y, far_y, rate_out, table, wind, raw, drift, sems):
     bx, by = field.shape[:2]
     copies = [pltpu.make_async_copy(value.at[x], raw.at[x], sems.at[x]) for x in range(bx)]
-    for copy in copies:
+    copies.append(pltpu.make_async_copy(drift_in, drift, sems.at[bx]))
+    for copy in copies[-1:] + copies[:-1]:
         copy.start()
     low = iota(1) < NW
     heading = iota(0)
@@ -155,11 +145,15 @@
         speed = (SPEED_BASE + index * SPEED_STEP) * (1.0 / SPACE_STEP)
         table[0, :, lanes(j)] = cosine * speed
         table[1, :, lanes(j)] = sine * speed
+    copies[bx].wait()
+    diagonal = lax.broadcasted_iota(jnp.int32, (by, by), 0) == lax.broadcasted_iota(
+        jnp.int32, (by, by), 1
+    )
     for x in range(bx):
         for d in range(2):
-            wind[d, x] = jnp.broadcast_to(
-                drift[x, :, d : d + 1] * (1.0 / SPACE_STEP), wind.shape[2:]
-            )
+            square = jnp.broadcast_to(drift[x, d : d + 1, :] * (1.0 / SPACE_STEP), (by, by))
+            column = jnp.sum(jnp.where(diagonal, square, 0.0), axis=1, keepdims=True)
+            wind[d, x] = jnp.broadcast_to(column, wind.shape[2:])
 
     moving = jnp.zeros(TILE, jnp.float32)
     for x in range(bx):
@@ -173,7 +167,7 @@
                 )
             return peak
 
-        moving = walk(by, 4, rate_of, moving)
+        moving = walk(by, rate_of, moving)
     turn = -1.0 + ((iota(1) % NW).astype(jnp.float32) + 0.5) * (2.0 / NW)
     turn_top = jnp.max(jnp.abs(turn), keepdims=True) / HEAD_STEP
     rate = jnp.max(moving, keepdims=True) + turn_top + TURN_LIMIT / TURN_STEP
@@ -189,47 +183,48 @@
             store(field, cells, x, y)
             return speed_gap(peak, cells, low)
 
-        peak = walk(by, 2, gap_of, peak)
+        peak = walk(by, gap_of, peak)
     row[...] = gap_row(peak, rate_row, low)
-    fill_edges(field, near, far, low_y, high_y)
-
-
-def slope_kernel(first, table, wind, near, far, from_low, from_high, center, limit, *refs):
+    fill_edges(field, near_x, far_x, near_y, far_y)
+
+
+def slope_kernel(first, table, wind, near_x, far_x, near_y, far_y, center, limit, *refs):
     parts, refs = refs[:5], refs[5:]
+    bx, by = center.shape[:2]
+    barrier, refs = refs[:bx], refs[bx:]
     if first:
-        barrier, kept, field, raw, sem = refs
-        fetch = pltpu.make_async_copy(limit, raw, sem)
+        kept, field, raw, sems = refs
+        targets = [raw.at[x] for x in range(bx)]
     else:
-        barrier, field, sem = refs
-        fetch = pltpu.make_async_copy(limit, barrier, sem)
-    fetch.start()
-    bx, by = center.shape[:2]
+        field, sems = refs
+        targets = barrier
+    fetches = [pltpu.make_async_copy(limit.at[x], targets[x], sems.at[x]) for x in range(bx)]
+    for fetch in fetches:
+        fetch.start()
     gx, gy = lax.axis_index("gx"), lax.axis_index("gy")
-    even = lax.rem(gx, 2) == 0
-    near_at = jnp.where(even, bx + 1, 0)
-    far_at = jnp.where(even, 0, bx + 1)
-
-    @pl.loop(0, by)
-    def _(y):
-        field[near_at, y + 1] = near[y]
-        field[far_at, y + 1] = far[y]
-        for x in range(bx):
+    for x in range(bx):
+        for y in range(by):
             field[x + 1, y + 1] = center[x, y]
-
-    @pl.loop(0, bx)
-    def _(x):
-        field[x + 1, 0] = from_low[x]
-        field[x + 1, by + 1] = from_high[x]
+    for index, size, near, far in ((gx, bx, near_x, far_x), (gy, by, near_y, far_y)):
+        even = lax.rem(index, 2) == 0
+        near_at = jnp.where(even, size + 1, 0)
+        far_at = jnp.where(even, 0, size + 1)
+        for i in range(near.shape[0]):
+            if near is near_x:
+                field[near_at, i + 1] = near[i]
+                field[far_at, i + 1] = far[i]
+            else:
+                field[i + 1, near_at] = near[i]
+                field[i + 1, far_at] = far[i]
 
     def extend(edge, along_x, at, end, inner):
         @pl.when(edge)
         def _():
-            @pl.loop(0, by if along_x else bx)
-            def _(i):
+            for i in range(1, (by if along_x else bx) + 1):
                 if along_x:
-                    field[at, i + 1] = 2.0 * field[end, i + 1] - field[inner, i + 1]
+                    field[at, i] = 2.0 * field[end, i] - field[inner, i]
                 else:
-                    field[i + 1, at] = 2.0 * field[i + 1, end] - field[i + 1, inner]
+                    field[i, at] = 2.0 * field[i, end] - field[i, inner]
 
     extend(gx == 0, True, 0, 1, 2)
     extend(gx == lax.axis_size("gx") - 1, True, bx + 1, bx, bx - 1)
@@ -282,25 +277,24 @@
                 parts[part][start + i, :, lanes(j)] = total
             return carry
 
-        walk(length, 2, slopes, 0)
-
-    fetch.wait()
+        walk(length, slopes, 0)
+
+    for fetch in fetches:
+        fetch.wait()
     if first:
+        keeps = []
         for x in range(bx):
-
-            def rearrange(y, carry, x=x):
-                store(barrier, apart(load(raw, x, y), low), x, y)
-                return carry
-
-            walk(by, 2, rearrange, 0)
-        keep = pltpu.make_async_copy(barrier, kept, sem)
-        keep.start()
-        keep.wait()
-
-
-def update_kernel(step, last, got, barrier, rate_row, steps_in, field_in, *refs):
-    parts, refs = refs[:5], refs[5:]
+            for y in range(by):
+                store(barrier[x], apart(load(raw, x, y), low), y)
+            keeps.append(pltpu.make_async_copy(barrier[x], kept.at[x], sems.at[x]))
+            keeps[-1].start()
+        for keep in keeps:
+            keep.wait()
+
+
+def update_kernel(step, last, got, rate_row, steps_in, field_in, *refs):
     bx, by = field_in.shape[:2]
+    parts, barrier, refs = refs[:5], refs[5 : 5 + bx], refs[5 + bx :]
     lane = lax.broadcasted_iota(jnp.int32, (1, LANES), 1)
     both = jnp.max(got[...], axis=0)
     gap = jnp.max(jnp.where(lane < NW, both, 0.0), keepdims=True)
@@ -314,14 +308,17 @@
     steps = jnp.where(lane == step, time_step, steps_in[...])
     low = iota(1) < NW
     if last:
-        value_out, steps_out, field_out, sems = refs
+        value_out, steps_out, field_out, steps_here, sems = refs
+    else:
+        field_out, near_x, far_x, near_y, far_y, row, steps_out = refs
+        steps_out[...] = steps
+
+    copies = []
+    if last:
         for i in range(ITERS):
-            steps_out[i] = steps[0, i]
-    else:
-        field_out, near, far, low_y, high_y, row, steps_out = refs
-        steps_out[...] = steps
-
-    copies = []
+            steps_here[i] = steps[0, i]
+        copies.append(pltpu.make_async_copy(steps_here, steps_out, sems.at[bx]))
+        copies[0].start()
     peak = jnp.zeros(TILE, jnp.float32)
     for part, start, x, y_start, length in runs(bx, by):
 
@@ -334,37 +331,46 @@
                 after, before = speed_sides(old, j, low, twice)
                 value = old[j] + weight * parts[part][start + i, :, lanes(j)]
                 value += weight_scaled * ((after + before) - twice)
-                cells.append(jnp.minimum(value, barrier[x, y, :, lanes(j)]))
+                cells.append(jnp.minimum(value, barrier[x][y, :, lanes(j)]))
             if last:
                 store(field_out, together(cells, low), x, y)
                 return peak
             store(field_out, cells, x, y)
             return speed_gap(peak, cells, low)
 
-        peak = walk(length, 4, update, peak)
+        peak = walk(length, update, peak)
         if last and y_start + length == by:
             copies.append(pltpu.make_async_copy(field_out.at[x], value_out.at[x], sems.at[x]))
             copies[-1].start()
-    for copy in copies:
-        copy.wait()
-    if not last:
+    if last:
+        for copy in copies:
+            copy.wait()
+    else:
         row[...] = gap_row(peak, rate_row[...], low)
-        fill_edges(field_out, near, far, low_y, high_y)
+        fill_edges(field_out, near_x, far_x, near_y, far_y)
 
 
 def hold(*arrays, space=pltpu.VMEM):
     return [pltpu.with_memory_space_constraint(a, space) for a in arrays]
 
 
-def swap(cells, axis, first):
-    count = lax.axis_size(axis)
-    pairs = [(i, (i + 1) % count) for i in range(first, count, 2)]
-    return lax.ppermute(cells, axis, pairs + [(j, i) for i, j in pairs])
-
-
-def shift(cells, axis, way):
-    count = lax.axis_size(axis)
-    return lax.ppermute(cells, axis, [(i, (i + way) % count) for i in range(count)])
+def swap(cells, along, first):
+    nx, ny = lax.axis_size("gx"), lax.axis_size("gy")
+    pairs = []
+    for x in range(nx):
+        for y in range(ny):
+            if along == "gx":
+                if (x - first) % 2 == 0 and (x + 1 < nx or first):
+                    pairs.append(((x, y), ((x + 1) % nx, y)))
+            elif y >= first and (y - first) % 2 == 0 and y + 1 < ny:
+                pairs.append(((x, y), (x, y + 1)))
+    paired = {i for pair in pairs for i in pair}
+    for x in range(0, nx - 1, 2):
+        for y in range(ny):
+            if not paired & {(x, y), (x + 1, y)}:
+                pairs.append(((x, y), (x + 1, y)))
+    links = [(i * ny + j, k * ny + m) for (i, j), (k, m) in pairs]
+    return lax.ppermute(cells, ("gx", "gy"), links + [(j, i) for i, j in links])
 
 
 def per_device(value_field, obstacle, drift_field):
@@ -381,7 +387,7 @@
     edges = parts[:4]
     row = in_vmem(1, LANES)
     in_hbm = jax.ShapeDtypeStruct(value_field.shape, jnp.float32)
-    vmem, smem, hbm = (pl.BlockSpec(memory_space=m) for m in (pltpu.VMEM, pltpu.SMEM, pltpu.HBM))
+    vmem, _, hbm = (pl.BlockSpec(memory_space=m) for m in (pltpu.VMEM, pltpu.SMEM, pltpu.HBM))
 
     def call(kernel, outs, *, out_specs=None, ins, in_specs=None, scratch=(), aliases={}):
         return pl.pallas_call(
@@ -398,12 +404,16 @@
         )(*ins)
 
     outs = [block, row, *edges, row, in_vmem(2, *cells), in_vmem(2, bx, by, LANES)]
-    field, sent, near, far, low_y, high_y, rate_row, table, wind = call(
+    field, sent, near_x, far_x, near_y, far_y, rate_row, table, wind = call(
         first_kernel,
         outs,
-        ins=[drift_field, *hold(value_field, space=pltpu.HBM)],
-        in_specs=[vmem, hbm],
-        scratch=[pltpu.VMEM(value_field.shape, jnp.float32), pltpu.SemaphoreType.DMA((bx,))],
+        ins=hold(drift_field.transpose(0, 2, 1), value_field, space=pltpu.HBM),
+        in_specs=[hbm, hbm],
+        scratch=[
+            pltpu.VMEM(value_field.shape, jnp.float32),
+            pltpu.VMEM((bx, 2, by), jnp.float32),
+            pltpu.SemaphoreType.DMA((bx + 1,)),
+        ],
     )
     steps = jnp.zeros((1, LANES), jnp.float32)
     (limit,) = hold(obstacle, space=pltpu.HBM)
@@ -411,47 +421,47 @@
 
     for step in range(ITERS):
         first, last = step == 0, step == ITERS - 1
-        got_edges = [
-            swap(near, "gx", 0),
-            swap(far, "gx", 1),
-            shift(high_y, "gy", 1),
-            shift(low_y, "gy", -1),
-        ]
+        got_far_x = swap(far_x, "gx", 1)
+        got_near_y = swap(near_y, "gy", 0)
+        got_far_y = swap(far_y, "gy", 1)
+        got_near_x = swap(near_x, "gx", 0)
+        got_edges = [got_near_x, got_far_x, got_near_y, got_far_y]
         rows = jnp.broadcast_to(sent[None], (devices, 1, LANES))
         got = lax.all_to_all(rows, ("gx", "gy"), 0, 0)
-        outs = [*parts, block] + [pltpu.HBM(value_field.shape, jnp.float32)] * first
+        outs = [*parts, *[in_vmem(by, *cells)] * bx] + [pltpu.HBM(value_field.shape, jnp.float32)] * first
         ins = [*hold(table, wind, *got_edges, field), limit]
         result = call(
             functools.partial(slope_kernel, first),
             outs,
-            out_specs=[vmem] * 6 + [hbm] * first,
+            out_specs=[vmem] * (5 + bx) + [hbm] * first,
             ins=ins,
             in_specs=[vmem] * 7 + [hbm],
             scratch=[padded]
             + [pltpu.VMEM(value_field.shape, jnp.float32)] * first
-            + [pltpu.SemaphoreType.DMA],
+            + [pltpu.SemaphoreType.DMA((bx,))],
             aliases={2 + i: i for i in range(4)},
         )
-        slopes, barrier = result[:5], result[5]
         if first:
-            (limit,) = hold(result[6], space=pltpu.HBM)
-        ins = hold(got, barrier, rate_row, steps, field, *slopes)
+            *result, limit = result
+            (limit,) = hold(limit, space=pltpu.HBM)
+        ins = hold(got, rate_row, steps, field, *result)
         if last:
             return call(
                 functools.partial(update_kernel, step, True),
                 [in_hbm, jax.ShapeDtypeStruct((ITERS,), jnp.float32)],
-                out_specs=[hbm, smem],
+                out_specs=[hbm, hbm],
                 ins=ins,
                 scratch=[
                     pltpu.VMEM(value_field.shape, jnp.float32),
-                    pltpu.SemaphoreType.DMA((bx,)),
+                    pltpu.SMEM((ITERS,), jnp.float32),
+                    pltpu.SemaphoreType.DMA((bx + 1,)),
                 ],
             )
-        field, near, far, low_y, high_y, sent, steps = call(
+        field, near_x, far_x, near_y, far_y, sent, steps = call(
             functools.partial(update_kernel, step, False),
             [block, *edges, row, row],
             ins=ins,
-            aliases={4: 0, **{5 + i: 1 + i for i in range(4)}},
+            aliases={3: 0, **{4 + i: 1 + i for i in range(4)}},
         )
 
 

time: 80.9 us -> 65.9 us (0.81)
  Pallas kernels: 28.3 us -> 14.3 us
  starting transfers between devices: 31.6 us -> 25.7 us
  waiting for transfers between devices: 16.8 us -> 22.3 us
    pallas_call x9, Pallas kernels: 28.3 us -> 14.3 us  [call(): pl.pallas_call(kernel, out_shape=tuple(outs), in_specs=in_specs or [vmem]...]
    ppermute x16, starting transfers between devices: 21.5 us -> 9.47 us  [swap(): return lax.ppermute(cells, ('gx', 'gy'), links + [(j, i) for i, j in links])]
    all_to_all x4, starting transfers between devices: 10.1 us -> 16.3 us  [per_device(): got = lax.all_to_all(rows, ('gx', 'gy'), 0, 0)]
    ppermute x16, waiting for transfers between devices: 6.74 us -> 10.1 us  [swap(): return lax.ppermute(cells, ('gx', 'gy'), links + [(j, i) for i, j in links])]
    all_to_all x4, waiting for transfers between devices: 10 us -> 12.2 us  [per_device(): got = lax.all_to_all(rows, ('gx', 'gy'), 0, 0)]
  transfers between devices with their start and end apart: 20 -> 20, of which waited for: 13 -> 11; matrix products, arithmetic and copies ran while one was open for 3% -> 4% of each run, Pallas kernels for 15% -> 10%
where the time goes in v2:
time: 65.9 us; the launch traced here: 65.6 us
  starting transfers between devices  25.7 us (39%)
  waiting for transfers between devices  22.3 us (34%)
  Pallas kernels  14.3 us (22%)
  local copies, waits for them, and re-layouts  2.42 us (4%)
  between operations  0.79 us (1%)
    all_to_all x4, starting transfers between devices, per_device(): got = lax.all_to_all(rows, ('gx', 'gy'), 0, 0)  16.3 us
    pallas_call x9, Pallas kernels, call(): pl.pallas_call(kernel, out_shape=tuple(outs), in_specs=in_specs or [vmem]...  14.3 us
    all_to_all x4, waiting for transfers between devices, per_device(): got = lax.all_to_all(rows, ('gx', 'gy'), 0, 0)  12.2 us
    ppermute x16, waiting for transfers between devices, swap(): return lax.ppermute(cells, ('gx', 'gy'), links + [(j, i) for i, j in links])  10.1 us
    ppermute x16, starting transfers between devices, swap(): return lax.ppermute(cells, ('gx', 'gy'), links + [(j, i) for i, j in links])  9.47 us
    broadcast_in_dim x4, local copies, waits for them, and re-layouts, per_device(): rows = jnp.broadcast_to(sent[None], (devices, 1, LANES))  2.42 us
  transfers between devices with their start and end apart: 20, of which 11 were waited for; matrix products, arithmetic and copies ran while one was open for 4% of the time, Pallas kernels for 10%

profile of v2, /device:TPU:0, one launch (start us, length us, event | category | flops | bytes accessed | tf_op | source)
XLA Modules:
  0.0 65.6 jit_solution(4645264397737551346)
XLA Ops:
  0.6 2.3 %shard_map.50 = (f32[4,8,8,1024]{3,2,1,0:T(8,128)S(1)}, f32[1,128]{1,0:T(1,128)S(1)}, f32[8,8,1024]{2,1,0:T(8,128)S(1)}, f32[8,8,1024]{2,1,0:T(8,128)S(1)}, f32[...) custom-call(f32[4,2,8]{2,1,0:T(2,128)} %bitcast.9, ...), custom_call_target="tpu_custom_call" | custom-call | flops 10485760 | bytes 4194304 | tf_op jit(solution)/shard_map/pallas_call | solution.py:393
  2.9 0.6 collective-permute-start
  3.5 3.5 %collective-permute-start.1 = (f32[8,8,1024]{2,1,0:T(8,128)S(1)}, f32[8,8,1024]{2,1,0:T(8,128)S(1)}, u32[]{:S(2)}, u32[]{:S(2)}) collective-permute-start(f32[8,8,1024]{2,1,0:T(8,128)S(1)} %get-tuple-element.75), channel_id=1, source_target_pairs={{4,8},{5,9},{6,10},{7,11},{12,16},{13,17},{14,18},{15,19},{20,24},... | collective-permute-start | bytes 786440 | tf_op jit(solution)/shard_map/ppermute | solution.py:373
  7.0 1.6 %collective-permute-start.2 = (f32[4,8,1024]{2,1,0:T(8,128)S(1)}, f32[4,8,1024]{2,1,0:T(8,128)S(1)}, u32[]{:S(2)}, u32[]{:S(2)}) collective-permute-start(f32[4,8,1024]{2,1,0:T(8,128)S(1)} %get-tuple-element.76), channel_id=1, source_target_pairs={{0,1},{2,3},{4,5},{6,7},{8,9},{10,11},{12,13},{14,15},{16,17},{18,... | collective-permute-start | bytes 393224 | tf_op jit(solution)/shard_map/ppermute | solution.py:373
  8.6 0.6 broadcast_in_dim.36
  9.2 3.5 %all-to-all-start = ((f32[32,1,128]{2,1,0:T(1,128)}), f32[32,1,128]{2,1,0:T(1,128)S(1)}, u32[]{:S(2)}, u32[]{:S(2)}) async-start(f32[32,1,128]{2,1,0:T(1,128)} %broadcast_in_dim.36), calls=%async_computation | async-start | bytes 32768 | tf_op jit(solution)/shard_map/all_to_all | solution.py:430
  13.1 2.4 %shard_map.51 = (f32[8,8,1024]{2,1,0:T(8,128)S(1)}, f32[8,8,1024]{2,1,0:T(8,128)S(1)}, f32[4,8,1024]{2,1,0:T(8,128)S(1)}, f32[4,8,1024]{2,1,0:T(8,128)S(1)}, f32...) custom-call(f32[2,8,1024]{2,1,0:T(8,128)S(1)} %get-tuple-element.72., ...), custom_call_target="tpu_custom_call", output_to_operand_aliasing={{0}: (2, {}), {1}: (3, {}), {2}: (4, {}), {3}: (5, {})} | custom-call | flops 10485760 | bytes 4194304 | tf_op jit(solution)/shard_map/pallas_call | solution.py:393
  15.5 4.4 %all-to-all-done.got = f32[32,1,128]{2,1,0:T(1,128)S(1)} async-done(((f32[32,1,128]{2,1,0:T(1,128)}), f32[32,1,128]{2,1,0:T(1,128)S(1)}, u32[]{:S(2)}, u32[]{:S(2)}) %all-to-all-start) | async-done | bytes 16416 | tf_op jit(solution)/shard_map/all_to_all | solution.py:430
  20.0 1.1 %shard_map.52 = (f32[4,8,8,1024]{3,2,1,0:T(8,128)S(1)}, f32[8,8,1024]{2,1,0:T(8,128)S(1)}, f32[8,8,1024]{2,1,0:T(8,128)S(1)}, f32[4,8,1024]{2,1,0:T(8,128)S(1)},...) custom-call(f32[32,1,128]{2,1,0:T(1,128)S(1)} %all-to-all-done.got, ...), custom_call_target="tpu_custom_call", output_to_operand_aliasing={{0}: (3, {}), {1}: (4, {}), {2}: (5, {}), {3}: (6, {}), {4}... | custom-call | flops 10485760 | bytes 4194304 | tf_op jit(solution)/shard_map/pallas_call | solution.py:393
  21.1 0.6 collective-permute-start.5
  21.8 0.5 collective-permute-start.6
  22.3 0.6 broadcast_in_dim.39
  22.9 4.2 %all-to-all-start.1 = ((f32[32,1,128]{2,1,0:T(1,128)}), f32[32,1,128]{2,1,0:T(1,128)S(1)}, u32[]{:S(2)}, u32[]{:S(2)}) async-start(f32[32,1,128]{2,1,0:T(1,128)} %broadcast_in_dim.39), calls=%async_computation.1 | async-start | bytes 32768 | tf_op jit(solution)/shard_map/all_to_all | solution.py:430
  27.3 3.1 %collective-permute-done.5.far_x = f32[8,8,1024]{2,1,0:T(8,128)S(1)} collective-permute-done((f32[8,8,1024]{2,1,0:T(8,128)S(1)}, f32[8,8,1024]{2,1,0:T(8,128)S(1)}, u32[]{:S(2)}, u32[]{:S(2)}) %collective-permute-start.5) | collective-permute-done | bytes 262176 | tf_op jit(solution)/shard_map/ppermute | solution.py:373
  30.5 1.3 %shard_map.53 = (f32[8,8,1024]{2,1,0:T(8,128)S(1)}, f32[8,8,1024]{2,1,0:T(8,128)S(1)}, f32[4,8,1024]{2,1,0:T(8,128)S(1)}, f32[4,8,1024]{2,1,0:T(8,128)S(1)}, f32...) custom-call(f32[2,8,1024]{2,1,0:T(8,128)S(1)} %get-tuple-element.72., ...), custom_call_target="tpu_custom_call", output_to_operand_aliasing={{0}: (2, {}), {1}: (3, {}), {2}: (4, {}), {3}: (5, {})} | custom-call | flops 10485760 | bytes 4194304 | tf_op jit(solution)/shard_map/pallas_call | solution.py:393
  31.8 2.6 %all-to-all-done.1.got = f32[32,1,128]{2,1,0:T(1,128)S(1)} async-done(((f32[32,1,128]{2,1,0:T(1,128)}), f32[32,1,128]{2,1,0:T(1,128)S(1)}, u32[]{:S(2)}, u32[]{:S(2)}) %all-to-all-start.1) | async-done | bytes 16416 | tf_op jit(solution)/shard_map/all_to_all | solution.py:430
  34.4 1.1 %shard_map.54 = (f32[4,8,8,1024]{3,2,1,0:T(8,128)S(1)}, f32[8,8,1024]{2,1,0:T(8,128)S(1)}, f32[8,8,1024]{2,1,0:T(8,128)S(1)}, f32[4,8,1024]{2,1,0:T(8,128)S(1)},...) custom-call(f32[32,1,128]{2,1,0:T(1,128)S(1)} %all-to-all-done.1.got, ...), custom_call_target="tpu_custom_call", output_to_operand_aliasing={{0}: (3, {}), {1}: (4, {}), {2}: (5, {}), {3}: (6, {}), {4}... | custom-call | flops 10485760 | bytes 4194304 | tf_op jit(solution)/shard_map/pallas_call | solution.py:393
  35.6 0.6 collective-permute-start.9
  36.2 0.5 collective-permute-start.10
  36.8 0.6 broadcast_in_dim.41
  37.4 4.2 %all-to-all-start.2 = ((f32[32,1,128]{2,1,0:T(1,128)}), f32[32,1,128]{2,1,0:T(1,128)S(1)}, u32[]{:S(2)}, u32[]{:S(2)}) async-start(f32[32,1,128]{2,1,0:T(1,128)} %broadcast_in_dim.41), calls=%async_computation.2 | async-start | bytes 32768 | tf_op jit(solution)/shard_map/all_to_all | solution.py:430
  41.8 3.1 %collective-permute-done.9.far_x = f32[8,8,1024]{2,1,0:T(8,128)S(1)} collective-permute-done((f32[8,8,1024]{2,1,0:T(8,128)S(1)}, f32[8,8,1024]{2,1,0:T(8,128)S(1)}, u32[]{:S(2)}, u32[]{:S(2)}) %collective-permute-start.9) | collective-permute-done | bytes 262176 | tf_op jit(solution)/shard_map/ppermute | solution.py:373
  44.9 1.3 %shard_map.55 = (f32[8,8,1024]{2,1,0:T(8,128)S(1)}, f32[8,8,1024]{2,1,0:T(8,128)S(1)}, f32[4,8,1024]{2,1,0:T(8,128)S(1)}, f32[4,8,1024]{2,1,0:T(8,128)S(1)}, f32...) custom-call(f32[2,8,1024]{2,1,0:T(8,128)S(1)} %get-tuple-element.72., ...), custom_call_target="tpu_custom_call", output_to_operand_aliasing={{0}: (2, {}), {1}: (3, {}), {2}: (4, {}), {3}: (5, {})} | custom-call | flops 10485760 | bytes 4194304 | tf_op jit(solution)/shard_map/pallas_call | solution.py:393
  46.2 2.6 %all-to-all-done.2.got = f32[32,1,128]{2,1,0:T(1,128)S(1)} async-done(((f32[32,1,128]{2,1,0:T(1,128)}), f32[32,1,128]{2,1,0:T(1,128)S(1)}, u32[]{:S(2)}, u32[]{:S(2)}) %all-to-all-start.2) | async-done | bytes 16416 | tf_op jit(solution)/shard_map/all_to_all | solution.py:430
  48.8 1.1 %shard_map.56 = (f32[4,8,8,1024]{3,2,1,0:T(8,128)S(1)}, f32[8,8,1024]{2,1,0:T(8,128)S(1)}, f32[8,8,1024]{2,1,0:T(8,128)S(1)}, f32[4,8,1024]{2,1,0:T(8,128)S(1)},...) custom-call(f32[32,1,128]{2,1,0:T(1,128)S(1)} %all-to-all-done.2.got, ...), custom_call_target="tpu_custom_call", output_to_operand_aliasing={{0}: (3, {}), {1}: (4, {}), {2}: (5, {}), {3}: (6, {}), {4}... | custom-call | flops 10485760 | bytes 4194304 | tf_op jit(solution)/shard_map/pallas_call | solution.py:393
  50.0 0.6 collective-permute-start.13
  51.2 0.6 broadcast_in_dim.43
  51.8 4.2 %all-to-all-start.3 = ((f32[32,1,128]{2,1,0:T(1,128)}), f32[32,1,128]{2,1,0:T(1,128)S(1)}, u32[]{:S(2)}, u32[]{:S(2)}) async-start(f32[32,1,128]{2,1,0:T(1,128)} %broadcast_in_dim.43), calls=%async_computation.3 | async-start | bytes 32768 | tf_op jit(solution)/shard_map/all_to_all | solution.py:430
  56.2 3.1 %collective-permute-done.13.far_x = f32[8,8,1024]{2,1,0:T(8,128)S(1)} collective-permute-done((f32[8,8,1024]{2,1,0:T(8,128)S(1)}, f32[8,8,1024]{2,1,0:T(8,128)S(1)}, u32[]{:S(2)}, u32[]{:S(2)}) %collective-permute-start.13) | collective-permute-done | bytes 262176 | tf_op jit(solution)/shard_map/ppermute | solution.py:373
  59.3 1.3 %shard_map.57 = (f32[8,8,1024]{2,1,0:T(8,128)S(1)}, f32[8,8,1024]{2,1,0:T(8,128)S(1)}, f32[4,8,1024]{2,1,0:T(8,128)S(1)}, f32[4,8,1024]{2,1,0:T(8,128)S(1)}, f32...) custom-call(f32[2,8,1024]{2,1,0:T(8,128)S(1)} %get-tuple-element.72., ...), custom_call_target="tpu_custom_call", output_to_operand_aliasing={{0}: (2, {}), {1}: (3, {}), {2}: (4, {}), {3}: (5, {})} | custom-call | flops 10485760 | bytes 4194304 | tf_op jit(solution)/shard_map/pallas_call | solution.py:393
  60.7 2.6 %all-to-all-done.3.got = f32[32,1,128]{2,1,0:T(1,128)S(1)} async-done(((f32[32,1,128]{2,1,0:T(1,128)}), f32[32,1,128]{2,1,0:T(1,128)S(1)}, u32[]{:S(2)}, u32[]{:S(2)}) %all-to-all-start.3) | async-done | bytes 16416 | tf_op jit(solution)/shard_map/all_to_all | solution.py:430
  63.3 2.3 %shard_map.58 = (f32[4,8,8,1024]{3,2,1,0:T(8,128)}, f32[4]{0:T(128)}) custom-call(f32[32,1,128]{2,1,0:T(1,128)S(1)} %all-to-all-done.3.got, f32[1,128]{1,0:T(1,128)S(1)} %get-tuple-element.70.rate_row, f32[1,128]{1,0:T(1,128)S(1)} %get-tuple-element.121.steps_in, f32[4,8,8,1024]{3,2,1,0:T(8,128)S(1)} %get-tuple-element.122.center.field_in, ...), custom_call_target="tpu_custom_call" | custom-call | flops 10485760 | bytes 4194304 | tf_op jit(solution)/shard_map/pallas_call | solution.py:393
  (22 shorter events, 1.4 us)
Async XLA Ops:
  2.9 9.8 %collective-permute-start = (f32[8,8,1024]{2,1,0:T(8,128)S(1)}, f32[8,8,1024]{2,1,0:T(8,128)S(1)}, u32[]{:S(2)}, u32[]{:S(2)}) collective-permute-start(f32[8,8,1024]{2,1,0:T(8,128)S(1)} %get-tuple-element.74), channel_id=1, source_target_pairs={{0,4},{1,5},{2,6},{3,7},{8,12},{9,13},{10,14},{11,15},{16,20},{17,... | collective-permute-start | bytes 786440 | tf_op jit(solution)/shard_map/ppermute | solution.py:373
  3.5 9.6 %collective-permute-start.1 = (f32[8,8,1024]{2,1,0:T(8,128)S(1)}, f32[8,8,1024]{2,1,0:T(8,128)S(1)}, u32[]{:S(2)}, u32[]{:S(2)}) collective-permute-start(f32[8,8,1024]{2,1,0:T(8,128)S(1)} %get-tuple-element.75), channel_id=1, source_target_pairs={{4,8},{5,9},{6,10},{7,11},{12,16},{13,17},{14,18},{15,19},{20,24},... | collective-permute-start | bytes 786440 | tf_op jit(solution)/shard_map/ppermute | solution.py:373
  7.0 5.7 %collective-permute-start.2 = (f32[4,8,1024]{2,1,0:T(8,128)S(1)}, f32[4,8,1024]{2,1,0:T(8,128)S(1)}, u32[]{:S(2)}, u32[]{:S(2)}) collective-permute-start(f32[4,8,1024]{2,1,0:T(8,128)S(1)} %get-tuple-element.76), channel_id=1, source_target_pairs={{0,1},{2,3},{4,5},{6,7},{8,9},{10,11},{12,13},{14,15},{16,17},{18,... | collective-permute-start | bytes 393224 | tf_op jit(solution)/shard_map/ppermute | solution.py:373
  8.6 4.1 %collective-permute-start.3 = (f32[4,8,1024]{2,1,0:T(8,128)S(1)}, f32[4,8,1024]{2,1,0:T(8,128)S(1)}, u32[]{:S(2)}, u32[]{:S(2)}) collective-permute-start(f32[4,8,1024]{2,1,0:T(8,128)S(1)} %get-tuple-element.77), channel_id=1, source_target_pairs={{1,2},{5,6},{9,10},{13,14},{17,18},{21,22},{25,26},{29,30},{0,4},{... | collective-permute-start | bytes 393224 | tf_op jit(solution)/shard_map/ppermute | solution.py:373
  9.2 10.7 %all-to-all-start = ((f32[32,1,128]{2,1,0:T(1,128)}), f32[32,1,128]{2,1,0:T(1,128)S(1)}, u32[]{:S(2)}, u32[]{:S(2)}) async-start(f32[32,1,128]{2,1,0:T(1,128)} %broadcast_in_dim.36), calls=%async_computation | async-start | bytes 32768 | tf_op jit(solution)/shard_map/all_to_all | solution.py:430
  21.1 6.2 %collective-permute-start.4 = (f32[8,8,1024]{2,1,0:T(8,128)S(1)}, f32[8,8,1024]{2,1,0:T(8,128)S(1)}, u32[]{:S(2)}, u32[]{:S(2)}) collective-permute-start(f32[8,8,1024]{2,1,0:T(8,128)S(1)} %get-tuple-element.90), channel_id=1, source_target_pairs={{0,4},{1,5},{2,6},{3,7},{8,12},{9,13},{10,14},{11,15},{16,20},{17,... | collective-permute-start | bytes 786440 | tf_op jit(solution)/shard_map/ppermute | solution.py:373
  21.1 9.3 %collective-permute-start.5 = (f32[8,8,1024]{2,1,0:T(8,128)S(1)}, f32[8,8,1024]{2,1,0:T(8,128)S(1)}, u32[]{:S(2)}, u32[]{:S(2)}) collective-permute-start(f32[8,8,1024]{2,1,0:T(8,128)S(1)} %get-tuple-element.91), channel_id=1, source_target_pairs={{4,8},{5,9},{6,10},{7,11},{12,16},{13,17},{14,18},{15,19},{20,24},... | collective-permute-start | bytes 786440 | tf_op jit(solution)/shard_map/ppermute | solution.py:373
  21.8 5.5 %collective-permute-start.6 = (f32[4,8,1024]{2,1,0:T(8,128)S(1)}, f32[4,8,1024]{2,1,0:T(8,128)S(1)}, u32[]{:S(2)}, u32[]{:S(2)}) collective-permute-start(f32[4,8,1024]{2,1,0:T(8,128)S(1)} %get-tuple-element.92), channel_id=1, source_target_pairs={{0,1},{2,3},{4,5},{6,7},{8,9},{10,11},{12,13},{14,15},{16,17},{18,... | collective-permute-start | bytes 393224 | tf_op jit(solution)/shard_map/ppermute | solution.py:373
  22.3 5.0 %collective-permute-start.7 = (f32[4,8,1024]{2,1,0:T(8,128)S(1)}, f32[4,8,1024]{2,1,0:T(8,128)S(1)}, u32[]{:S(2)}, u32[]{:S(2)}) collective-permute-start(f32[4,8,1024]{2,1,0:T(8,128)S(1)} %get-tuple-element.93), channel_id=1, source_target_pairs={{1,2},{5,6},{9,10},{13,14},{17,18},{21,22},{25,26},{29,30},{0,4},{... | collective-permute-start | bytes 393224 | tf_op jit(solution)/shard_map/ppermute | solution.py:373
  22.9 11.5 %all-to-all-start.1 = ((f32[32,1,128]{2,1,0:T(1,128)}), f32[32,1,128]{2,1,0:T(1,128)S(1)}, u32[]{:S(2)}, u32[]{:S(2)}) async-start(f32[32,1,128]{2,1,0:T(1,128)} %broadcast_in_dim.39), calls=%async_computation.1 | async-start | bytes 32768 | tf_op jit(solution)/shard_map/all_to_all | solution.py:430
  35.5 6.2 %collective-permute-start.8 = (f32[8,8,1024]{2,1,0:T(8,128)S(1)}, f32[8,8,1024]{2,1,0:T(8,128)S(1)}, u32[]{:S(2)}, u32[]{:S(2)}) collective-permute-start(f32[8,8,1024]{2,1,0:T(8,128)S(1)} %get-tuple-element.107), channel_id=1, source_target_pairs={{0,4},{1,5},{2,6},{3,7},{8,12},{9,13},{10,14},{11,15},{16,20},{17,... | collective-permute-start | bytes 786440 | tf_op jit(solution)/shard_map/ppermute | solution.py:373
  35.6 9.3 %collective-permute-start.9 = (f32[8,8,1024]{2,1,0:T(8,128)S(1)}, f32[8,8,1024]{2,1,0:T(8,128)S(1)}, u32[]{:S(2)}, u32[]{:S(2)}) collective-permute-start(f32[8,8,1024]{2,1,0:T(8,128)S(1)} %get-tuple-element.108), channel_id=1, source_target_pairs={{4,8},{5,9},{6,10},{7,11},{12,16},{13,17},{14,18},{15,19},{20,24},... | collective-permute-start | bytes 786440 | tf_op jit(solution)/shard_map/ppermute | solution.py:373
  36.2 5.5 %collective-permute-start.10 = (f32[4,8,1024]{2,1,0:T(8,128)S(1)}, f32[4,8,1024]{2,1,0:T(8,128)S(1)}, u32[]{:S(2)}, u32[]{:S(2)}) collective-permute-start(f32[4,8,1024]{2,1,0:T(8,128)S(1)} %get-tuple-element.109), channel_id=1, source_target_pairs={{0,1},{2,3},{4,5},{6,7},{8,9},{10,11},{12,13},{14,15},{16,17},{18,... | collective-permute-start | bytes 393224 | tf_op jit(solution)/shard_map/ppermute | solution.py:373
  36.8 5.0 %collective-permute-start.11 = (f32[4,8,1024]{2,1,0:T(8,128)S(1)}, f32[4,8,1024]{2,1,0:T(8,128)S(1)}, u32[]{:S(2)}, u32[]{:S(2)}) collective-permute-start(f32[4,8,1024]{2,1,0:T(8,128)S(1)} %get-tuple-element.110), channel_id=1, source_target_pairs={{1,2},{5,6},{9,10},{13,14},{17,18},{21,22},{25,26},{29,30},{0,4},{... | collective-permute-start | bytes 393224 | tf_op jit(solution)/shard_map/ppermute | solution.py:373
  37.4 11.5 %all-to-all-start.2 = ((f32[32,1,128]{2,1,0:T(1,128)}), f32[32,1,128]{2,1,0:T(1,128)S(1)}, u32[]{:S(2)}, u32[]{:S(2)}) async-start(f32[32,1,128]{2,1,0:T(1,128)} %broadcast_in_dim.41), calls=%async_computation.2 | async-start | bytes 32768 | tf_op jit(solution)/shard_map/all_to_all | solution.py:430
  49.9 6.2 %collective-permute-start.12 = (f32[8,8,1024]{2,1,0:T(8,128)S(1)}, f32[8,8,1024]{2,1,0:T(8,128)S(1)}, u32[]{:S(2)}, u32[]{:S(2)}) collective-permute-start(f32[8,8,1024]{2,1,0:T(8,128)S(1)} %get-tuple-element.123), channel_id=1, source_target_pairs={{0,4},{1,5},{2,6},{3,7},{8,12},{9,13},{10,14},{11,15},{16,20},{17,... | collective-permute-start | bytes 786440 | tf_op jit(solution)/shard_map/ppermute | solution.py:373
  50.0 9.3 %collective-permute-start.13 = (f32[8,8,1024]{2,1,0:T(8,128)S(1)}, f32[8,8,1024]{2,1,0:T(8,128)S(1)}, u32[]{:S(2)}, u32[]{:S(2)}) collective-permute-start(f32[8,8,1024]{2,1,0:T(8,128)S(1)} %get-tuple-element.124), channel_id=1, source_target_pairs={{4,8},{5,9},{6,10},{7,11},{12,16},{13,17},{14,18},{15,19},{20,24},... | collective-permute-start | bytes 786440 | tf_op jit(solution)/shard_map/ppermute | solution.py:373
  50.7 5.5 %collective-permute-start.14 = (f32[4,8,1024]{2,1,0:T(8,128)S(1)}, f32[4,8,1024]{2,1,0:T(8,128)S(1)}, u32[]{:S(2)}, u32[]{:S(2)}) collective-permute-start(f32[4,8,1024]{2,1,0:T(8,128)S(1)} %get-tuple-element.125), channel_id=1, source_target_pairs={{0,1},{2,3},{4,5},{6,7},{8,9},{10,11},{12,13},{14,15},{16,17},{18,... | collective-permute-start | bytes 393224 | tf_op jit(solution)/shard_map/ppermute | solution.py:373
  51.2 5.0 %collective-permute-start.15 = (f32[4,8,1024]{2,1,0:T(8,128)S(1)}, f32[4,8,1024]{2,1,0:T(8,128)S(1)}, u32[]{:S(2)}, u32[]{:S(2)}) collective-permute-start(f32[4,8,1024]{2,1,0:T(8,128)S(1)} %get-tuple-element.126), channel_id=1, source_target_pairs={{1,2},{5,6},{9,10},{13,14},{17,18},{21,22},{25,26},{29,30},{0,4},{... | collective-permute-start | bytes 393224 | tf_op jit(solution)/shard_map/ppermute | solution.py:373
  51.8 11.5 %all-to-all-start.3 = ((f32[32,1,128]{2,1,0:T(1,128)}), f32[32,1,128]{2,1,0:T(1,128)S(1)}, u32[]{:S(2)}, u32[]{:S(2)}) async-start(f32[32,1,128]{2,1,0:T(1,128)} %broadcast_in_dim.43), calls=%async_computation.3 | async-start | bytes 32768 | tf_op jit(solution)/shard_map/all_to_all | solution.py:430

commit v3 on v2

--- a/solution.py
+++ b/solution.py
@@ -317,7 +317,7 @@
     if last:
         for i in range(ITERS):
             steps_here[i] = steps[0, i]
-        copies.append(pltpu.make_async_copy(steps_here, steps_out, sems.at[bx]))
+        copies.append(pltpu.make_async_copy(steps_here, steps_out, sems.at[0]))
         copies[0].start()
     peak = jnp.zeros(TILE, jnp.float32)
     for part, start, x, y_start, length in runs(bx, by):
@@ -339,8 +339,13 @@
             return speed_gap(peak, cells, low)
 
         peak = walk(length, update, peak)
-        if last and y_start + length == by:
-            copies.append(pltpu.make_async_copy(field_out.at[x], value_out.at[x], sems.at[x]))
+        if last:
+            ys = pl.ds(y_start, length)
+            copies.append(
+                pltpu.make_async_copy(
+                    field_out.at[x, ys], value_out.at[x, ys], sems.at[len(copies)]
+                )
+            )
             copies[-1].start()
     if last:
         for copy in copies:
@@ -454,7 +459,7 @@
                 scratch=[
                     pltpu.VMEM(value_field.shape, jnp.float32),
                     pltpu.SMEM((ITERS,), jnp.float32),
-                    pltpu.SemaphoreType.DMA((bx + 1,)),
+                    pltpu.SemaphoreType.DMA((1 + len(runs(bx, by)),)),
                 ],
             )
         field, near_x, far_x, near_y, far_y, sent, steps = call(

time: 65.9 us -> 65.9 us (level)
  no operation moved by 1% of the time
where the time goes in v3:
time: 65.9 us; the launch traced here: 65.6 us
  starting transfers between devices  25.7 us (39%)
  waiting for transfers between devices  22.3 us (34%)
  Pallas kernels  14.3 us (22%)
  local copies, waits for them, and re-layouts  2.42 us (4%)
  between operations  0.79 us (1%)
    all_to_all x4, starting transfers between devices, per_device(): got = lax.all_to_all(rows, ('gx', 'gy'), 0, 0)  16.3 us
    pallas_call x9, Pallas kernels, call(): pl.pallas_call(kernel, out_shape=tuple(outs), in_specs=in_specs or [vmem]...  14.3 us
    all_to_all x4, waiting for transfers between devices, per_device(): got = lax.all_to_all(rows, ('gx', 'gy'), 0, 0)  12.2 us
    ppermute x16, waiting for transfers between devices, swap(): return lax.ppermute(cells, ('gx', 'gy'), links + [(j, i) for i, j in links])  10.1 us
    ppermute x16, starting transfers between devices, swap(): return lax.ppermute(cells, ('gx', 'gy'), links + [(j, i) for i, j in links])  9.47 us
    broadcast_in_dim x4, local copies, waits for them, and re-layouts, per_device(): rows = jnp.broadcast_to(sent[None], (devices, 1, LANES))  2.42 us
  transfers between devices with their start and end apart: 20, of which 11 were waited for; matrix products, arithmetic and copies ran while one was open for 4% of the time, Pallas kernels for 10%

profile of v3, /device:TPU:0, one launch (start us, length us, event | category | flops | bytes accessed | tf_op | source)
XLA Modules:
  0.0 65.6 jit_solution(7522264803614925405)
XLA Ops:
  0.6 2.3 %shard_map.50 = (f32[4,8,8,1024]{3,2,1,0:T(8,128)S(1)}, f32[1,128]{1,0:T(1,128)S(1)}, f32[8,8,1024]{2,1,0:T(8,128)S(1)}, f32[8,8,1024]{2,1,0:T(8,128)S(1)}, f32[...) custom-call(f32[4,2,8]{2,1,0:T(2,128)} %bitcast.9, ...), custom_call_target="tpu_custom_call" | custom-call | flops 10485760 | bytes 4194304 | tf_op jit(solution)/shard_map/pallas_call | solution.py:398
  2.9 0.6 collective-permute-start
  3.5 3.5 %collective-permute-start.1 = (f32[8,8,1024]{2,1,0:T(8,128)S(1)}, f32[8,8,1024]{2,1,0:T(8,128)S(1)}, u32[]{:S(2)}, u32[]{:S(2)}) collective-permute-start(f32[8,8,1024]{2,1,0:T(8,128)S(1)} %get-tuple-element.75), channel_id=1, source_target_pairs={{4,8},{5,9},{6,10},{7,11},{12,16},{13,17},{14,18},{15,19},{20,24},... | collective-permute-start | bytes 786440 | tf_op jit(solution)/shard_map/ppermute | solution.py:378
  7.0 1.6 %collective-permute-start.2 = (f32[4,8,1024]{2,1,0:T(8,128)S(1)}, f32[4,8,1024]{2,1,0:T(8,128)S(1)}, u32[]{:S(2)}, u32[]{:S(2)}) collective-permute-start(f32[4,8,1024]{2,1,0:T(8,128)S(1)} %get-tuple-element.76), channel_id=1, source_target_pairs={{0,1},{2,3},{4,5},{6,7},{8,9},{10,11},{12,13},{14,15},{16,17},{18,... | collective-permute-start | bytes 393224 | tf_op jit(solution)/shard_map/ppermute | solution.py:378
  8.6 0.6 broadcast_in_dim.36
  9.2 3.5 %all-to-all-start = ((f32[32,1,128]{2,1,0:T(1,128)}), f32[32,1,128]{2,1,0:T(1,128)S(1)}, u32[]{:S(2)}, u32[]{:S(2)}) async-start(f32[32,1,128]{2,1,0:T(1,128)} %broadcast_in_dim.36), calls=%async_computation | async-start | bytes 32768 | tf_op jit(solution)/shard_map/all_to_all | solution.py:435
  13.1 2.4 %shard_map.51 = (f32[8,8,1024]{2,1,0:T(8,128)S(1)}, f32[8,8,1024]{2,1,0:T(8,128)S(1)}, f32[4,8,1024]{2,1,0:T(8,128)S(1)}, f32[4,8,1024]{2,1,0:T(8,128)S(1)}, f32...) custom-call(f32[2,8,1024]{2,1,0:T(8,128)S(1)} %get-tuple-element.72., ...), custom_call_target="tpu_custom_call", output_to_operand_aliasing={{0}: (2, {}), {1}: (3, {}), {2}: (4, {}), {3}: (5, {})} | custom-call | flops 10485760 | bytes 4194304 | tf_op jit(solution)/shard_map/pallas_call | solution.py:398
  15.5 4.4 %all-to-all-done.got = f32[32,1,128]{2,1,0:T(1,128)S(1)} async-done(((f32[32,1,128]{2,1,0:T(1,128)}), f32[32,1,128]{2,1,0:T(1,128)S(1)}, u32[]{:S(2)}, u32[]{:S(2)}) %all-to-all-start) | async-done | bytes 16416 | tf_op jit(solution)/shard_map/all_to_all | solution.py:435
  20.0 1.1 %shard_map.52 = (f32[4,8,8,1024]{3,2,1,0:T(8,128)S(1)}, f32[8,8,1024]{2,1,0:T(8,128)S(1)}, f32[8,8,1024]{2,1,0:T(8,128)S(1)}, f32[4,8,1024]{2,1,0:T(8,128)S(1)},...) custom-call(f32[32,1,128]{2,1,0:T(1,128)S(1)} %all-to-all-done.got, ...), custom_call_target="tpu_custom_call", output_to_operand_aliasing={{0}: (3, {}), {1}: (4, {}), {2}: (5, {}), {3}: (6, {}), {4}... | custom-call | flops 10485760 | bytes 4194304 | tf_op jit(solution)/shard_map/pallas_call | solution.py:398
  21.1 0.6 collective-permute-start.5
  21.8 0.5 collective-permute-start.6
  22.3 0.6 broadcast_in_dim.39
  22.9 4.2 %all-to-all-start.1 = ((f32[32,1,128]{2,1,0:T(1,128)}), f32[32,1,128]{2,1,0:T(1,128)S(1)}, u32[]{:S(2)}, u32[]{:S(2)}) async-start(f32[32,1,128]{2,1,0:T(1,128)} %broadcast_in_dim.39), calls=%async_computation.1 | async-start | bytes 32768 | tf_op jit(solution)/shard_map/all_to_all | solution.py:435
  27.3 3.1 %collective-permute-done.5.far_x = f32[8,8,1024]{2,1,0:T(8,128)S(1)} collective-permute-done((f32[8,8,1024]{2,1,0:T(8,128)S(1)}, f32[8,8,1024]{2,1,0:T(8,128)S(1)}, u32[]{:S(2)}, u32[]{:S(2)}) %collective-permute-start.5) | collective-permute-done | bytes 262176 | tf_op jit(solution)/shard_map/ppermute | solution.py:378
  30.5 1.3 %shard_map.53 = (f32[8,8,1024]{2,1,0:T(8,128)S(1)}, f32[8,8,1024]{2,1,0:T(8,128)S(1)}, f32[4,8,1024]{2,1,0:T(8,128)S(1)}, f32[4,8,1024]{2,1,0:T(8,128)S(1)}, f32...) custom-call(f32[2,8,1024]{2,1,0:T(8,128)S(1)} %get-tuple-element.72., ...), custom_call_target="tpu_custom_call", output_to_operand_aliasing={{0}: (2, {}), {1}: (3, {}), {2}: (4, {}), {3}: (5, {})} | custom-call | flops 10485760 | bytes 4194304 | tf_op jit(solution)/shard_map/pallas_call | solution.py:398
  31.8 2.6 %all-to-all-done.1.got = f32[32,1,128]{2,1,0:T(1,128)S(1)} async-done(((f32[32,1,128]{2,1,0:T(1,128)}), f32[32,1,128]{2,1,0:T(1,128)S(1)}, u32[]{:S(2)}, u32[]{:S(2)}) %all-to-all-start.1) | async-done | bytes 16416 | tf_op jit(solution)/shard_map/all_to_all | solution.py:435
  34.4 1.1 %shard_map.54 = (f32[4,8,8,1024]{3,2,1,0:T(8,128)S(1)}, f32[8,8,1024]{2,1,0:T(8,128)S(1)}, f32[8,8,1024]{2,1,0:T(8,128)S(1)}, f32[4,8,1024]{2,1,0:T(8,128)S(1)},...) custom-call(f32[32,1,128]{2,1,0:T(1,128)S(1)} %all-to-all-done.1.got, ...), custom_call_target="tpu_custom_call", output_to_operand_aliasing={{0}: (3, {}), {1}: (4, {}), {2}: (5, {}), {3}: (6, {}), {4}... | custom-call | flops 10485760 | bytes 4194304 | tf_op jit(solution)/shard_map/pallas_call | solution.py:398
  35.6 0.6 collective-permute-start.9
  36.2 0.5 collective-permute-start.10
  36.8 0.6 broadcast_in_dim.41
  37.4 4.2 %all-to-all-start.2 = ((f32[32,1,128]{2,1,0:T(1,128)}), f32[32,1,128]{2,1,0:T(1,128)S(1)}, u32[]{:S(2)}, u32[]{:S(2)}) async-start(f32[32,1,128]{2,1,0:T(1,128)} %broadcast_in_dim.41), calls=%async_computation.2 | async-start | bytes 32768 | tf_op jit(solution)/shard_map/all_to_all | solution.py:435
  41.8 3.1 %collective-permute-done.9.far_x = f32[8,8,1024]{2,1,0:T(8,128)S(1)} collective-permute-done((f32[8,8,1024]{2,1,0:T(8,128)S(1)}, f32[8,8,1024]{2,1,0:T(8,128)S(1)}, u32[]{:S(2)}, u32[]{:S(2)}) %collective-permute-start.9) | collective-permute-done | bytes 262176 | tf_op jit(solution)/shard_map/ppermute | solution.py:378
  44.9 1.3 %shard_map.55 = (f32[8,8,1024]{2,1,0:T(8,128)S(1)}, f32[8,8,1024]{2,1,0:T(8,128)S(1)}, f32[4,8,1024]{2,1,0:T(8,128)S(1)}, f32[4,8,1024]{2,1,0:T(8,128)S(1)}, f32...) custom-call(f32[2,8,1024]{2,1,0:T(8,128)S(1)} %get-tuple-element.72., ...), custom_call_target="tpu_custom_call", output_to_operand_aliasing={{0}: (2, {}), {1}: (3, {}), {2}: (4, {}), {3}: (5, {})} | custom-call | flops 10485760 | bytes 4194304 | tf_op jit(solution)/shard_map/pallas_call | solution.py:398
  46.2 2.6 %all-to-all-done.2.got = f32[32,1,128]{2,1,0:T(1,128)S(1)} async-done(((f32[32,1,128]{2,1,0:T(1,128)}), f32[32,1,128]{2,1,0:T(1,128)S(1)}, u32[]{:S(2)}, u32[]{:S(2)}) %all-to-all-start.2) | async-done | bytes 16416 | tf_op jit(solution)/shard_map/all_to_all | solution.py:435
  48.8 1.1 %shard_map.56 = (f32[4,8,8,1024]{3,2,1,0:T(8,128)S(1)}, f32[8,8,1024]{2,1,0:T(8,128)S(1)}, f32[8,8,1024]{2,1,0:T(8,128)S(1)}, f32[4,8,1024]{2,1,0:T(8,128)S(1)},...) custom-call(f32[32,1,128]{2,1,0:T(1,128)S(1)} %all-to-all-done.2.got, ...), custom_call_target="tpu_custom_call", output_to_operand_aliasing={{0}: (3, {}), {1}: (4, {}), {2}: (5, {}), {3}: (6, {}), {4}... | custom-call | flops 10485760 | bytes 4194304 | tf_op jit(solution)/shard_map/pallas_call | solution.py:398
  50.0 0.6 collective-permute-start.13
  51.2 0.6 broadcast_in_dim.43
  51.8 4.2 %all-to-all-start.3 = ((f32[32,1,128]{2,1,0:T(1,128)}), f32[32,1,128]{2,1,0:T(1,128)S(1)}, u32[]{:S(2)}, u32[]{:S(2)}) async-start(f32[32,1,128]{2,1,0:T(1,128)} %broadcast_in_dim.43), calls=%async_computation.3 | async-start | bytes 32768 | tf_op jit(solution)/shard_map/all_to_all | solution.py:435
  56.2 3.1 %collective-permute-done.13.far_x = f32[8,8,1024]{2,1,0:T(8,128)S(1)} collective-permute-done((f32[8,8,1024]{2,1,0:T(8,128)S(1)}, f32[8,8,1024]{2,1,0:T(8,128)S(1)}, u32[]{:S(2)}, u32[]{:S(2)}) %collective-permute-start.13) | collective-permute-done | bytes 262176 | tf_op jit(solution)/shard_map/ppermute | solution.py:378
  59.3 1.3 %shard_map.57 = (f32[8,8,1024]{2,1,0:T(8,128)S(1)}, f32[8,8,1024]{2,1,0:T(8,128)S(1)}, f32[4,8,1024]{2,1,0:T(8,128)S(1)}, f32[4,8,1024]{2,1,0:T(8,128)S(1)}, f32...) custom-call(f32[2,8,1024]{2,1,0:T(8,128)S(1)} %get-tuple-element.72., ...), custom_call_target="tpu_custom_call", output_to_operand_aliasing={{0}: (2, {}), {1}: (3, {}), {2}: (4, {}), {3}: (5, {})} | custom-call | flops 10485760 | bytes 4194304 | tf_op jit(solution)/shard_map/pallas_call | solution.py:398
  60.7 2.6 %all-to-all-done.3.got = f32[32,1,128]{2,1,0:T(1,128)S(1)} async-done(((f32[32,1,128]{2,1,0:T(1,128)}), f32[32,1,128]{2,1,0:T(1,128)S(1)}, u32[]{:S(2)}, u32[]{:S(2)}) %all-to-all-start.3) | async-done | bytes 16416 | tf_op jit(solution)/shard_map/all_to_all | solution.py:435
  63.3 2.3 %shard_map.58 = (f32[4,8,8,1024]{3,2,1,0:T(8,128)}, f32[4]{0:T(128)}) custom-call(f32[32,1,128]{2,1,0:T(1,128)S(1)} %all-to-all-done.3.got, f32[1,128]{1,0:T(1,128)S(1)} %get-tuple-element.70.rate_row, f32[1,128]{1,0:T(1,128)S(1)} %get-tuple-element.121.steps_in, f32[4,8,8,1024]{3,2,1,0:T(8,128)S(1)} %get-tuple-element.122.center.field_in, ...), custom_call_target="tpu_custom_call" | custom-call | flops 10485760 | bytes 4194304 | tf_op jit(solution)/shard_map/pallas_call | solution.py:398
  (22 shorter events, 1.4 us)
Async XLA Ops:
  2.9 9.8 %collective-permute-start = (f32[8,8,1024]{2,1,0:T(8,128)S(1)}, f32[8,8,1024]{2,1,0:T(8,128)S(1)}, u32[]{:S(2)}, u32[]{:S(2)}) collective-permute-start(f32[8,8,1024]{2,1,0:T(8,128)S(1)} %get-tuple-element.74), channel_id=1, source_target_pairs={{0,4},{1,5},{2,6},{3,7},{8,12},{9,13},{10,14},{11,15},{16,20},{17,... | collective-permute-start | bytes 786440 | tf_op jit(solution)/shard_map/ppermute | solution.py:378
  3.5 9.6 %collective-permute-start.1 = (f32[8,8,1024]{2,1,0:T(8,128)S(1)}, f32[8,8,1024]{2,1,0:T(8,128)S(1)}, u32[]{:S(2)}, u32[]{:S(2)}) collective-permute-start(f32[8,8,1024]{2,1,0:T(8,128)S(1)} %get-tuple-element.75), channel_id=1, source_target_pairs={{4,8},{5,9},{6,10},{7,11},{12,16},{13,17},{14,18},{15,19},{20,24},... | collective-permute-start | bytes 786440 | tf_op jit(solution)/shard_map/ppermute | solution.py:378
  7.0 5.7 %collective-permute-start.2 = (f32[4,8,1024]{2,1,0:T(8,128)S(1)}, f32[4,8,1024]{2,1,0:T(8,128)S(1)}, u32[]{:S(2)}, u32[]{:S(2)}) collective-permute-start(f32[4,8,1024]{2,1,0:T(8,128)S(1)} %get-tuple-element.76), channel_id=1, source_target_pairs={{0,1},{2,3},{4,5},{6,7},{8,9},{10,11},{12,13},{14,15},{16,17},{18,... | collective-permute-start | bytes 393224 | tf_op jit(solution)/shard_map/ppermute | solution.py:378
  8.6 4.1 %collective-permute-start.3 = (f32[4,8,1024]{2,1,0:T(8,128)S(1)}, f32[4,8,1024]{2,1,0:T(8,128)S(1)}, u32[]{:S(2)}, u32[]{:S(2)}) collective-permute-start(f32[4,8,1024]{2,1,0:T(8,128)S(1)} %get-tuple-element.77), channel_id=1, source_target_pairs={{1,2},{5,6},{9,10},{13,14},{17,18},{21,22},{25,26},{29,30},{0,4},{... | collective-permute-start | bytes 393224 | tf_op jit(solution)/shard_map/ppermute | solution.py:378
  9.2 10.7 %all-to-all-start = ((f32[32,1,128]{2,1,0:T(1,128)}), f32[32,1,128]{2,1,0:T(1,128)S(1)}, u32[]{:S(2)}, u32[]{:S(2)}) async-start(f32[32,1,128]{2,1,0:T(1,128)} %broadcast_in_dim.36), calls=%async_computation | async-start | bytes 32768 | tf_op jit(solution)/shard_map/all_to_all | solution.py:435
  21.1 6.2 %collective-permute-start.4 = (f32[8,8,1024]{2,1,0:T(8,128)S(1)}, f32[8,8,1024]{2,1,0:T(8,128)S(1)}, u32[]{:S(2)}, u32[]{:S(2)}) collective-permute-start(f32[8,8,1024]{2,1,0:T(8,128)S(1)} %get-tuple-element.90), channel_id=1, source_target_pairs={{0,4},{1,5},{2,6},{3,7},{8,12},{9,13},{10,14},{11,15},{16,20},{17,... | collective-permute-start | bytes 786440 | tf_op jit(solution)/shard_map/ppermute | solution.py:378
  21.1 9.3 %collective-permute-start.5 = (f32[8,8,1024]{2,1,0:T(8,128)S(1)}, f32[8,8,1024]{2,1,0:T(8,128)S(1)}, u32[]{:S(2)}, u32[]{:S(2)}) collective-permute-start(f32[8,8,1024]{2,1,0:T(8,128)S(1)} %get-tuple-element.91), channel_id=1, source_target_pairs={{4,8},{5,9},{6,10},{7,11},{12,16},{13,17},{14,18},{15,19},{20,24},... | collective-permute-start | bytes 786440 | tf_op jit(solution)/shard_map/ppermute | solution.py:378
  21.8 5.5 %collective-permute-start.6 = (f32[4,8,1024]{2,1,0:T(8,128)S(1)}, f32[4,8,1024]{2,1,0:T(8,128)S(1)}, u32[]{:S(2)}, u32[]{:S(2)}) collective-permute-start(f32[4,8,1024]{2,1,0:T(8,128)S(1)} %get-tuple-element.92), channel_id=1, source_target_pairs={{0,1},{2,3},{4,5},{6,7},{8,9},{10,11},{12,13},{14,15},{16,17},{18,... | collective-permute-start | bytes 393224 | tf_op jit(solution)/shard_map/ppermute | solution.py:378
  22.3 5.0 %collective-permute-start.7 = (f32[4,8,1024]{2,1,0:T(8,128)S(1)}, f32[4,8,1024]{2,1,0:T(8,128)S(1)}, u32[]{:S(2)}, u32[]{:S(2)}) collective-permute-start(f32[4,8,1024]{2,1,0:T(8,128)S(1)} %get-tuple-element.93), channel_id=1, source_target_pairs={{1,2},{5,6},{9,10},{13,14},{17,18},{21,22},{25,26},{29,30},{0,4},{... | collective-permute-start | bytes 393224 | tf_op jit(solution)/shard_map/ppermute | solution.py:378
  22.9 11.5 %all-to-all-start.1 = ((f32[32,1,128]{2,1,0:T(1,128)}), f32[32,1,128]{2,1,0:T(1,128)S(1)}, u32[]{:S(2)}, u32[]{:S(2)}) async-start(f32[32,1,128]{2,1,0:T(1,128)} %broadcast_in_dim.39), calls=%async_computation.1 | async-start | bytes 32768 | tf_op jit(solution)/shard_map/all_to_all | solution.py:435
  35.5 6.2 %collective-permute-start.8 = (f32[8,8,1024]{2,1,0:T(8,128)S(1)}, f32[8,8,1024]{2,1,0:T(8,128)S(1)}, u32[]{:S(2)}, u32[]{:S(2)}) collective-permute-start(f32[8,8,1024]{2,1,0:T(8,128)S(1)} %get-tuple-element.107), channel_id=1, source_target_pairs={{0,4},{1,5},{2,6},{3,7},{8,12},{9,13},{10,14},{11,15},{16,20},{17,... | collective-permute-start | bytes 786440 | tf_op jit(solution)/shard_map/ppermute | solution.py:378
  35.6 9.3 %collective-permute-start.9 = (f32[8,8,1024]{2,1,0:T(8,128)S(1)}, f32[8,8,1024]{2,1,0:T(8,128)S(1)}, u32[]{:S(2)}, u32[]{:S(2)}) collective-permute-start(f32[8,8,1024]{2,1,0:T(8,128)S(1)} %get-tuple-element.108), channel_id=1, source_target_pairs={{4,8},{5,9},{6,10},{7,11},{12,16},{13,17},{14,18},{15,19},{20,24},... | collective-permute-start | bytes 786440 | tf_op jit(solution)/shard_map/ppermute | solution.py:378
  36.2 5.5 %collective-permute-start.10 = (f32[4,8,1024]{2,1,0:T(8,128)S(1)}, f32[4,8,1024]{2,1,0:T(8,128)S(1)}, u32[]{:S(2)}, u32[]{:S(2)}) collective-permute-start(f32[4,8,1024]{2,1,0:T(8,128)S(1)} %get-tuple-element.109), channel_id=1, source_target_pairs={{0,1},{2,3},{4,5},{6,7},{8,9},{10,11},{12,13},{14,15},{16,17},{18,... | collective-permute-start | bytes 393224 | tf_op jit(solution)/shard_map/ppermute | solution.py:378
  36.8 5.0 %collective-permute-start.11 = (f32[4,8,1024]{2,1,0:T(8,128)S(1)}, f32[4,8,1024]{2,1,0:T(8,128)S(1)}, u32[]{:S(2)}, u32[]{:S(2)}) collective-permute-start(f32[4,8,1024]{2,1,0:T(8,128)S(1)} %get-tuple-element.110), channel_id=1, source_target_pairs={{1,2},{5,6},{9,10},{13,14},{17,18},{21,22},{25,26},{29,30},{0,4},{... | collective-permute-start | bytes 393224 | tf_op jit(solution)/shard_map/ppermute | solution.py:378
  37.4 11.5 %all-to-all-start.2 = ((f32[32,1,128]{2,1,0:T(1,128)}), f32[32,1,128]{2,1,0:T(1,128)S(1)}, u32[]{:S(2)}, u32[]{:S(2)}) async-start(f32[32,1,128]{2,1,0:T(1,128)} %broadcast_in_dim.41), calls=%async_computation.2 | async-start | bytes 32768 | tf_op jit(solution)/shard_map/all_to_all | solution.py:435
  49.9 6.2 %collective-permute-start.12 = (f32[8,8,1024]{2,1,0:T(8,128)S(1)}, f32[8,8,1024]{2,1,0:T(8,128)S(1)}, u32[]{:S(2)}, u32[]{:S(2)}) collective-permute-start(f32[8,8,1024]{2,1,0:T(8,128)S(1)} %get-tuple-element.123), channel_id=1, source_target_pairs={{0,4},{1,5},{2,6},{3,7},{8,12},{9,13},{10,14},{11,15},{16,20},{17,... | collective-permute-start | bytes 786440 | tf_op jit(solution)/shard_map/ppermute | solution.py:378
  50.0 9.3 %collective-permute-start.13 = (f32[8,8,1024]{2,1,0:T(8,128)S(1)}, f32[8,8,1024]{2,1,0:T(8,128)S(1)}, u32[]{:S(2)}, u32[]{:S(2)}) collective-permute-start(f32[8,8,1024]{2,1,0:T(8,128)S(1)} %get-tuple-element.124), channel_id=1, source_target_pairs={{4,8},{5,9},{6,10},{7,11},{12,16},{13,17},{14,18},{15,19},{20,24},... | collective-permute-start | bytes 786440 | tf_op jit(solution)/shard_map/ppermute | solution.py:378
  50.7 5.5 %collective-permute-start.14 = (f32[4,8,1024]{2,1,0:T(8,128)S(1)}, f32[4,8,1024]{2,1,0:T(8,128)S(1)}, u32[]{:S(2)}, u32[]{:S(2)}) collective-permute-start(f32[4,8,1024]{2,1,0:T(8,128)S(1)} %get-tuple-element.125), channel_id=1, source_target_pairs={{0,1},{2,3},{4,5},{6,7},{8,9},{10,11},{12,13},{14,15},{16,17},{18,... | collective-permute-start | bytes 393224 | tf_op jit(solution)/shard_map/ppermute | solution.py:378
  51.2 5.0 %collective-permute-start.15 = (f32[4,8,1024]{2,1,0:T(8,128)S(1)}, f32[4,8,1024]{2,1,0:T(8,128)S(1)}, u32[]{:S(2)}, u32[]{:S(2)}) collective-permute-start(f32[4,8,1024]{2,1,0:T(8,128)S(1)} %get-tuple-element.126), channel_id=1, source_target_pairs={{1,2},{5,6},{9,10},{13,14},{17,18},{21,22},{25,26},{29,30},{0,4},{... | collective-permute-start | bytes 393224 | tf_op jit(solution)/shard_map/ppermute | solution.py:378
  51.8 11.5 %all-to-all-start.3 = ((f32[32,1,128]{2,1,0:T(1,128)}), f32[32,1,128]{2,1,0:T(1,128)S(1)}, u32[]{:S(2)}, u32[]{:S(2)}) async-start(f32[32,1,128]{2,1,0:T(1,128)} %broadcast_in_dim.43), calls=%async_computation.3 | async-start | bytes 32768 | tf_op jit(solution)/shard_map/all_to_all | solution.py:435

commit v4 on v3

--- a/solution.py
+++ b/solution.py
@@ -160,7 +160,7 @@
 
         def rate_of(y, peak, x=x):
             east, north = wind_at(wind, x, y)
-            for j in range(SLABS):
+            for j in (0, SLABS - 1):
                 peak = jnp.maximum(
                     peak,
                     jnp.abs(table[0, :, lanes(j)] + east) + jnp.abs(table[1, :, lanes(j)] + north),
@@ -239,6 +239,7 @@
     turn_first = lane % NW == 0
     turn_last = lane % NW == NW - 1
 
+    keeps = []
     for part, start, x, y_start, length in runs(bx, by):
 
         def slopes(i, carry, part=part, start=start, x=x, y_start=y_start):
@@ -277,19 +278,20 @@
                 parts[part][start + i, :, lanes(j)] = total
             return carry
 
+        if first and x == bx - 1 and y_start + length == by:
+            for k in range(bx):
+                fetches[k].wait()
+                for y in range(by):
+                    store(barrier[k], apart(load(raw, k, y), low), y)
+                keeps.append(pltpu.make_async_copy(barrier[k], kept.at[k], sems.at[k]))
+                keeps[-1].start()
         walk(length, slopes, 0)
 
-    for fetch in fetches:
-        fetch.wait()
-    if first:
-        keeps = []
-        for x in range(bx):
-            for y in range(by):
-                store(barrier[x], apart(load(raw, x, y), low), y)
-            keeps.append(pltpu.make_async_copy(barrier[x], kept.at[x], sems.at[x]))
-            keeps[-1].start()
-        for keep in keeps:
-            keep.wait()
+    if not first:
+        for fetch in fetches:
+            fetch.wait()
+    for keep in keeps:
+        keep.wait()
 
 
 def update_kernel(step, last, got, rate_row, steps_in, field_in, *refs):
@@ -314,11 +316,6 @@
         steps_out[...] = steps
 
     copies = []
-    if last:
-        for i in range(ITERS):
-            steps_here[i] = steps[0, i]
-        copies.append(pltpu.make_async_copy(steps_here, steps_out, sems.at[0]))
-        copies[0].start()
     peak = jnp.zeros(TILE, jnp.float32)
     for part, start, x, y_start, length in runs(bx, by):
 
@@ -348,6 +345,10 @@
             )
             copies[-1].start()
     if last:
+        for i in range(ITERS):
+            steps_here[i] = steps[0, i]
+        copies.append(pltpu.make_async_copy(steps_here, steps_out, sems.at[len(copies)]))
+        copies[-1].start()
         for copy in copies:
             copy.wait()
     else:

time: 65.9 us -> 65.6 us (level)
  no operation moved by 1% of the time
where the time goes in v4:
time: 65.6 us; the launch traced here: 65.3 us
  starting transfers between devices  25.7 us (39%)
  waiting for transfers between devices  22.4 us (34%)
  Pallas kernels  14 us (21%)
  local copies, waits for them, and re-layouts  2.42 us (4%)
  between operations  0.79 us (1%)
    all_to_all x4, starting transfers between devices, per_device(): got = lax.all_to_all(rows, ('gx', 'gy'), 0, 0)  16.3 us
    pallas_call x9, Pallas kernels, call(): pl.pallas_call(kernel, out_shape=tuple(outs), in_specs=in_specs or [vmem]...  14 us
    all_to_all x4, waiting for transfers between devices, per_device(): got = lax.all_to_all(rows, ('gx', 'gy'), 0, 0)  12.4 us
    ppermute x16, waiting for transfers between devices, swap(): return lax.ppermute(cells, ('gx', 'gy'), links + [(j, i) for i, j in links])  10.1 us
    ppermute x16, starting transfers between devices, swap(): return lax.ppermute(cells, ('gx', 'gy'), links + [(j, i) for i, j in links])  9.47 us
    broadcast_in_dim x4, local copies, waits for them, and re-layouts, per_device(): rows = jnp.broadcast_to(sent[None], (devices, 1, LANES))  2.42 us
  transfers between devices with their start and end apart: 20, of which 11 were waited for; matrix products, arithmetic and copies ran while one was open for 4% of the time, Pallas kernels for 10%

profile of v4, /device:TPU:0, one launch (start us, length us, event | category | flops | bytes accessed | tf_op | source)
XLA Modules:
  0.0 65.3 jit_solution(12929567864696036358)
XLA Ops:
  0.6 2.1 %shard_map.50 = (f32[4,8,8,1024]{3,2,1,0:T(8,128)S(1)}, f32[1,128]{1,0:T(1,128)S(1)}, f32[8,8,1024]{2,1,0:T(8,128)S(1)}, f32[8,8,1024]{2,1,0:T(8,128)S(1)}, f32[...) custom-call(f32[4,2,8]{2,1,0:T(2,128)} %bitcast.9, ...), custom_call_target="tpu_custom_call" | custom-call | flops 10485760 | bytes 4194304 | tf_op jit(solution)/shard_map/pallas_call | solution.py:399
  2.8 0.6 collective-permute-start
  3.3 3.5 %collective-permute-start.1 = (f32[8,8,1024]{2,1,0:T(8,128)S(1)}, f32[8,8,1024]{2,1,0:T(8,128)S(1)}, u32[]{:S(2)}, u32[]{:S(2)}) collective-permute-start(f32[8,8,1024]{2,1,0:T(8,128)S(1)} %get-tuple-element.75), channel_id=1, source_target_pairs={{4,8},{5,9},{6,10},{7,11},{12,16},{13,17},{14,18},{15,19},{20,24},... | collective-permute-start | bytes 786440 | tf_op jit(solution)/shard_map/ppermute | solution.py:379
  6.9 1.6 %collective-permute-start.2 = (f32[4,8,1024]{2,1,0:T(8,128)S(1)}, f32[4,8,1024]{2,1,0:T(8,128)S(1)}, u32[]{:S(2)}, u32[]{:S(2)}) collective-permute-start(f32[4,8,1024]{2,1,0:T(8,128)S(1)} %get-tuple-element.76), channel_id=1, source_target_pairs={{0,1},{2,3},{4,5},{6,7},{8,9},{10,11},{12,13},{14,15},{16,17},{18,... | collective-permute-start | bytes 393224 | tf_op jit(solution)/shard_map/ppermute | solution.py:379
  8.4 0.6 broadcast_in_dim.36
  9.0 3.5 %all-to-all-start = ((f32[32,1,128]{2,1,0:T(1,128)}), f32[32,1,128]{2,1,0:T(1,128)S(1)}, u32[]{:S(2)}, u32[]{:S(2)}) async-start(f32[32,1,128]{2,1,0:T(1,128)} %broadcast_in_dim.36), calls=%async_computation | async-start | bytes 32768 | tf_op jit(solution)/shard_map/all_to_all | solution.py:436
  12.9 2.3 %shard_map.51 = (f32[8,8,1024]{2,1,0:T(8,128)S(1)}, f32[8,8,1024]{2,1,0:T(8,128)S(1)}, f32[4,8,1024]{2,1,0:T(8,128)S(1)}, f32[4,8,1024]{2,1,0:T(8,128)S(1)}, f32...) custom-call(f32[2,8,1024]{2,1,0:T(8,128)S(1)} %get-tuple-element.72., ...), custom_call_target="tpu_custom_call", output_to_operand_aliasing={{0}: (2, {}), {1}: (3, {}), {2}: (4, {}), {3}: (5, {})} | custom-call | flops 10485760 | bytes 4194304 | tf_op jit(solution)/shard_map/pallas_call | solution.py:399
  15.2 4.6 %all-to-all-done.got = f32[32,1,128]{2,1,0:T(1,128)S(1)} async-done(((f32[32,1,128]{2,1,0:T(1,128)}), f32[32,1,128]{2,1,0:T(1,128)S(1)}, u32[]{:S(2)}, u32[]{:S(2)}) %all-to-all-start) | async-done | bytes 16416 | tf_op jit(solution)/shard_map/all_to_all | solution.py:436
  19.8 1.1 %shard_map.52 = (f32[4,8,8,1024]{3,2,1,0:T(8,128)S(1)}, f32[8,8,1024]{2,1,0:T(8,128)S(1)}, f32[8,8,1024]{2,1,0:T(8,128)S(1)}, f32[4,8,1024]{2,1,0:T(8,128)S(1)},...) custom-call(f32[32,1,128]{2,1,0:T(1,128)S(1)} %all-to-all-done.got, ...), custom_call_target="tpu_custom_call", output_to_operand_aliasing={{0}: (3, {}), {1}: (4, {}), {2}: (5, {}), {3}: (6, {}), {4}... | custom-call | flops 10485760 | bytes 4194304 | tf_op jit(solution)/shard_map/pallas_call | solution.py:399
  20.9 0.6 collective-permute-start.5
  21.6 0.5 collective-permute-start.6
  22.1 0.6 broadcast_in_dim.39
  22.7 4.2 %all-to-all-start.1 = ((f32[32,1,128]{2,1,0:T(1,128)}), f32[32,1,128]{2,1,0:T(1,128)S(1)}, u32[]{:S(2)}, u32[]{:S(2)}) async-start(f32[32,1,128]{2,1,0:T(1,128)} %broadcast_in_dim.39), calls=%async_computation.1 | async-start | bytes 32768 | tf_op jit(solution)/shard_map/all_to_all | solution.py:436
  27.1 3.1 %collective-permute-done.5.far_x = f32[8,8,1024]{2,1,0:T(8,128)S(1)} collective-permute-done((f32[8,8,1024]{2,1,0:T(8,128)S(1)}, f32[8,8,1024]{2,1,0:T(8,128)S(1)}, u32[]{:S(2)}, u32[]{:S(2)}) %collective-permute-start.5) | collective-permute-done | bytes 262176 | tf_op jit(solution)/shard_map/ppermute | solution.py:379
  30.3 1.3 %shard_map.53 = (f32[8,8,1024]{2,1,0:T(8,128)S(1)}, f32[8,8,1024]{2,1,0:T(8,128)S(1)}, f32[4,8,1024]{2,1,0:T(8,128)S(1)}, f32[4,8,1024]{2,1,0:T(8,128)S(1)}, f32...) custom-call(f32[2,8,1024]{2,1,0:T(8,128)S(1)} %get-tuple-element.72., ...), custom_call_target="tpu_custom_call", output_to_operand_aliasing={{0}: (2, {}), {1}: (3, {}), {2}: (4, {}), {3}: (5, {})} | custom-call | flops 10485760 | bytes 4194304 | tf_op jit(solution)/shard_map/pallas_call | solution.py:399
  31.6 2.6 %all-to-all-done.1.got = f32[32,1,128]{2,1,0:T(1,128)S(1)} async-done(((f32[32,1,128]{2,1,0:T(1,128)}), f32[32,1,128]{2,1,0:T(1,128)S(1)}, u32[]{:S(2)}, u32[]{:S(2)}) %all-to-all-start.1) | async-done | bytes 16416 | tf_op jit(solution)/shard_map/all_to_all | solution.py:436
  34.2 1.1 %shard_map.54 = (f32[4,8,8,1024]{3,2,1,0:T(8,128)S(1)}, f32[8,8,1024]{2,1,0:T(8,128)S(1)}, f32[8,8,1024]{2,1,0:T(8,128)S(1)}, f32[4,8,1024]{2,1,0:T(8,128)S(1)},...) custom-call(f32[32,1,128]{2,1,0:T(1,128)S(1)} %all-to-all-done.1.got, ...), custom_call_target="tpu_custom_call", output_to_operand_aliasing={{0}: (3, {}), {1}: (4, {}), {2}: (5, {}), {3}: (6, {}), {4}... | custom-call | flops 10485760 | bytes 4194304 | tf_op jit(solution)/shard_map/pallas_call | solution.py:399
  35.4 0.6 collective-permute-start.9
  36.0 0.5 collective-permute-start.10
  36.6 0.6 broadcast_in_dim.41
  37.2 4.2 %all-to-all-start.2 = ((f32[32,1,128]{2,1,0:T(1,128)}), f32[32,1,128]{2,1,0:T(1,128)S(1)}, u32[]{:S(2)}, u32[]{:S(2)}) async-start(f32[32,1,128]{2,1,0:T(1,128)} %broadcast_in_dim.41), calls=%async_computation.2 | async-start | bytes 32768 | tf_op jit(solution)/shard_map/all_to_all | solution.py:436
  41.6 3.1 %collective-permute-done.9.far_x = f32[8,8,1024]{2,1,0:T(8,128)S(1)} collective-permute-done((f32[8,8,1024]{2,1,0:T(8,128)S(1)}, f32[8,8,1024]{2,1,0:T(8,128)S(1)}, u32[]{:S(2)}, u32[]{:S(2)}) %collective-permute-start.9) | collective-permute-done | bytes 262176 | tf_op jit(solution)/shard_map/ppermute | solution.py:379
  44.7 1.3 %shard_map.55 = (f32[8,8,1024]{2,1,0:T(8,128)S(1)}, f32[8,8,1024]{2,1,0:T(8,128)S(1)}, f32[4,8,1024]{2,1,0:T(8,128)S(1)}, f32[4,8,1024]{2,1,0:T(8,128)S(1)}, f32...) custom-call(f32[2,8,1024]{2,1,0:T(8,128)S(1)} %get-tuple-element.72., ...), custom_call_target="tpu_custom_call", output_to_operand_aliasing={{0}: (2, {}), {1}: (3, {}), {2}: (4, {}), {3}: (5, {})} | custom-call | flops 10485760 | bytes 4194304 | tf_op jit(solution)/shard_map/pallas_call | solution.py:399
  46.0 2.6 %all-to-all-done.2.got = f32[32,1,128]{2,1,0:T(1,128)S(1)} async-done(((f32[32,1,128]{2,1,0:T(1,128)}), f32[32,1,128]{2,1,0:T(1,128)S(1)}, u32[]{:S(2)}, u32[]{:S(2)}) %all-to-all-start.2) | async-done | bytes 16416 | tf_op jit(solution)/shard_map/all_to_all | solution.py:436
  48.6 1.1 %shard_map.56 = (f32[4,8,8,1024]{3,2,1,0:T(8,128)S(1)}, f32[8,8,1024]{2,1,0:T(8,128)S(1)}, f32[8,8,1024]{2,1,0:T(8,128)S(1)}, f32[4,8,1024]{2,1,0:T(8,128)S(1)},...) custom-call(f32[32,1,128]{2,1,0:T(1,128)S(1)} %all-to-all-done.2.got, ...), custom_call_target="tpu_custom_call", output_to_operand_aliasing={{0}: (3, {}), {1}: (4, {}), {2}: (5, {}), {3}: (6, {}), {4}... | custom-call | flops 10485760 | bytes 4194304 | tf_op jit(solution)/shard_map/pallas_call | solution.py:399
  49.8 0.6 collective-permute-start.13
  51.0 0.6 broadcast_in_dim.43
  51.6 4.2 %all-to-all-start.3 = ((f32[32,1,128]{2,1,0:T(1,128)}), f32[32,1,128]{2,1,0:T(1,128)S(1)}, u32[]{:S(2)}, u32[]{:S(2)}) async-start(f32[32,1,128]{2,1,0:T(1,128)} %broadcast_in_dim.43), calls=%async_computation.3 | async-start | bytes 32768 | tf_op jit(solution)/shard_map/all_to_all | solution.py:436
  56.0 3.1 %collective-permute-done.13.far_x = f32[8,8,1024]{2,1,0:T(8,128)S(1)} collective-permute-done((f32[8,8,1024]{2,1,0:T(8,128)S(1)}, f32[8,8,1024]{2,1,0:T(8,128)S(1)}, u32[]{:S(2)}, u32[]{:S(2)}) %collective-permute-start.13) | collective-permute-done | bytes 262176 | tf_op jit(solution)/shard_map/ppermute | solution.py:379
  59.1 1.3 %shard_map.57 = (f32[8,8,1024]{2,1,0:T(8,128)S(1)}, f32[8,8,1024]{2,1,0:T(8,128)S(1)}, f32[4,8,1024]{2,1,0:T(8,128)S(1)}, f32[4,8,1024]{2,1,0:T(8,128)S(1)}, f32...) custom-call(f32[2,8,1024]{2,1,0:T(8,128)S(1)} %get-tuple-element.72., ...), custom_call_target="tpu_custom_call", output_to_operand_aliasing={{0}: (2, {}), {1}: (3, {}), {2}: (4, {}), {3}: (5, {})} | custom-call | flops 10485760 | bytes 4194304 | tf_op jit(solution)/shard_map/pallas_call | solution.py:399
  60.5 2.6 %all-to-all-done.3.got = f32[32,1,128]{2,1,0:T(1,128)S(1)} async-done(((f32[32,1,128]{2,1,0:T(1,128)}), f32[32,1,128]{2,1,0:T(1,128)S(1)}, u32[]{:S(2)}, u32[]{:S(2)}) %all-to-all-start.3) | async-done | bytes 16416 | tf_op jit(solution)/shard_map/all_to_all | solution.py:436
  63.1 2.2 %shard_map.58 = (f32[4,8,8,1024]{3,2,1,0:T(8,128)}, f32[4]{0:T(128)}) custom-call(f32[32,1,128]{2,1,0:T(1,128)S(1)} %all-to-all-done.3.got, f32[1,128]{1,0:T(1,128)S(1)} %get-tuple-element.70.rate_row, f32[1,128]{1,0:T(1,128)S(1)} %get-tuple-element.121.steps_in, f32[4,8,8,1024]{3,2,1,0:T(8,128)S(1)} %get-tuple-element.122.center.field_in, ...), custom_call_target="tpu_custom_call" | custom-call | flops 10485760 | bytes 4194304 | tf_op jit(solution)/shard_map/pallas_call | solution.py:399
  (22 shorter events, 1.4 us)
Async XLA Ops:
  2.8 9.8 %collective-permute-start = (f32[8,8,1024]{2,1,0:T(8,128)S(1)}, f32[8,8,1024]{2,1,0:T(8,128)S(1)}, u32[]{:S(2)}, u32[]{:S(2)}) collective-permute-start(f32[8,8,1024]{2,1,0:T(8,128)S(1)} %get-tuple-element.74), channel_id=1, source_target_pairs={{0,4},{1,5},{2,6},{3,7},{8,12},{9,13},{10,14},{11,15},{16,20},{17,... | collective-permute-start | bytes 786440 | tf_op jit(solution)/shard_map/ppermute | solution.py:379
  3.3 9.6 %collective-permute-start.1 = (f32[8,8,1024]{2,1,0:T(8,128)S(1)}, f32[8,8,1024]{2,1,0:T(8,128)S(1)}, u32[]{:S(2)}, u32[]{:S(2)}) collective-permute-start(f32[8,8,1024]{2,1,0:T(8,128)S(1)} %get-tuple-element.75), channel_id=1, source_target_pairs={{4,8},{5,9},{6,10},{7,11},{12,16},{13,17},{14,18},{15,19},{20,24},... | collective-permute-start | bytes 786440 | tf_op jit(solution)/shard_map/ppermute | solution.py:379
  6.9 5.7 %collective-permute-start.2 = (f32[4,8,1024]{2,1,0:T(8,128)S(1)}, f32[4,8,1024]{2,1,0:T(8,128)S(1)}, u32[]{:S(2)}, u32[]{:S(2)}) collective-permute-start(f32[4,8,1024]{2,1,0:T(8,128)S(1)} %get-tuple-element.76), channel_id=1, source_target_pairs={{0,1},{2,3},{4,5},{6,7},{8,9},{10,11},{12,13},{14,15},{16,17},{18,... | collective-permute-start | bytes 393224 | tf_op jit(solution)/shard_map/ppermute | solution.py:379
  8.4 4.1 %collective-permute-start.3 = (f32[4,8,1024]{2,1,0:T(8,128)S(1)}, f32[4,8,1024]{2,1,0:T(8,128)S(1)}, u32[]{:S(2)}, u32[]{:S(2)}) collective-permute-start(f32[4,8,1024]{2,1,0:T(8,128)S(1)} %get-tuple-element.77), channel_id=1, source_target_pairs={{1,2},{5,6},{9,10},{13,14},{17,18},{21,22},{25,26},{29,30},{0,4},{... | collective-permute-start | bytes 393224 | tf_op jit(solution)/shard_map/ppermute | solution.py:379
  9.0 10.7 %all-to-all-start = ((f32[32,1,128]{2,1,0:T(1,128)}), f32[32,1,128]{2,1,0:T(1,128)S(1)}, u32[]{:S(2)}, u32[]{:S(2)}) async-start(f32[32,1,128]{2,1,0:T(1,128)} %broadcast_in_dim.36), calls=%async_computation | async-start | bytes 32768 | tf_op jit(solution)/shard_map/all_to_all | solution.py:436
  20.9 6.2 %collective-permute-start.4 = (f32[8,8,1024]{2,1,0:T(8,128)S(1)}, f32[8,8,1024]{2,1,0:T(8,128)S(1)}, u32[]{:S(2)}, u32[]{:S(2)}) collective-permute-start(f32[8,8,1024]{2,1,0:T(8,128)S(1)} %get-tuple-element.90), channel_id=1, source_target_pairs={{0,4},{1,5},{2,6},{3,7},{8,12},{9,13},{10,14},{11,15},{16,20},{17,... | collective-permute-start | bytes 786440 | tf_op jit(solution)/shard_map/ppermute | solution.py:379
  20.9 9.3 %collective-permute-start.5 = (f32[8,8,1024]{2,1,0:T(8,128)S(1)}, f32[8,8,1024]{2,1,0:T(8,128)S(1)}, u32[]{:S(2)}, u32[]{:S(2)}) collective-permute-start(f32[8,8,1024]{2,1,0:T(8,128)S(1)} %get-tuple-element.91), channel_id=1, source_target_pairs={{4,8},{5,9},{6,10},{7,11},{12,16},{13,17},{14,18},{15,19},{20,24},... | collective-permute-start | bytes 786440 | tf_op jit(solution)/shard_map/ppermute | solution.py:379
  21.6 5.5 %collective-permute-start.6 = (f32[4,8,1024]{2,1,0:T(8,128)S(1)}, f32[4,8,1024]{2,1,0:T(8,128)S(1)}, u32[]{:S(2)}, u32[]{:S(2)}) collective-permute-start(f32[4,8,1024]{2,1,0:T(8,128)S(1)} %get-tuple-element.92), channel_id=1, source_target_pairs={{0,1},{2,3},{4,5},{6,7},{8,9},{10,11},{12,13},{14,15},{16,17},{18,... | collective-permute-start | bytes 393224 | tf_op jit(solution)/shard_map/ppermute | solution.py:379
  22.1 5.0 %collective-permute-start.7 = (f32[4,8,1024]{2,1,0:T(8,128)S(1)}, f32[4,8,1024]{2,1,0:T(8,128)S(1)}, u32[]{:S(2)}, u32[]{:S(2)}) collective-permute-start(f32[4,8,1024]{2,1,0:T(8,128)S(1)} %get-tuple-element.93), channel_id=1, source_target_pairs={{1,2},{5,6},{9,10},{13,14},{17,18},{21,22},{25,26},{29,30},{0,4},{... | collective-permute-start | bytes 393224 | tf_op jit(solution)/shard_map/ppermute | solution.py:379
  22.7 11.5 %all-to-all-start.1 = ((f32[32,1,128]{2,1,0:T(1,128)}), f32[32,1,128]{2,1,0:T(1,128)S(1)}, u32[]{:S(2)}, u32[]{:S(2)}) async-start(f32[32,1,128]{2,1,0:T(1,128)} %broadcast_in_dim.39), calls=%async_computation.1 | async-start | bytes 32768 | tf_op jit(solution)/shard_map/all_to_all | solution.py:436
  35.3 6.2 %collective-permute-start.8 = (f32[8,8,1024]{2,1,0:T(8,128)S(1)}, f32[8,8,1024]{2,1,0:T(8,128)S(1)}, u32[]{:S(2)}, u32[]{:S(2)}) collective-permute-start(f32[8,8,1024]{2,1,0:T(8,128)S(1)} %get-tuple-element.107), channel_id=1, source_target_pairs={{0,4},{1,5},{2,6},{3,7},{8,12},{9,13},{10,14},{11,15},{16,20},{17,... | collective-permute-start | bytes 786440 | tf_op jit(solution)/shard_map/ppermute | solution.py:379
  35.4 9.3 %collective-permute-start.9 = (f32[8,8,1024]{2,1,0:T(8,128)S(1)}, f32[8,8,1024]{2,1,0:T(8,128)S(1)}, u32[]{:S(2)}, u32[]{:S(2)}) collective-permute-start(f32[8,8,1024]{2,1,0:T(8,128)S(1)} %get-tuple-element.108), channel_id=1, source_target_pairs={{4,8},{5,9},{6,10},{7,11},{12,16},{13,17},{14,18},{15,19},{20,24},... | collective-permute-start | bytes 786440 | tf_op jit(solution)/shard_map/ppermute | solution.py:379
  36.0 5.5 %collective-permute-start.10 = (f32[4,8,1024]{2,1,0:T(8,128)S(1)}, f32[4,8,1024]{2,1,0:T(8,128)S(1)}, u32[]{:S(2)}, u32[]{:S(2)}) collective-permute-start(f32[4,8,1024]{2,1,0:T(8,128)S(1)} %get-tuple-element.109), channel_id=1, source_target_pairs={{0,1},{2,3},{4,5},{6,7},{8,9},{10,11},{12,13},{14,15},{16,17},{18,... | collective-permute-start | bytes 393224 | tf_op jit(solution)/shard_map/ppermute | solution.py:379
  36.6 5.0 %collective-permute-start.11 = (f32[4,8,1024]{2,1,0:T(8,128)S(1)}, f32[4,8,1024]{2,1,0:T(8,128)S(1)}, u32[]{:S(2)}, u32[]{:S(2)}) collective-permute-start(f32[4,8,1024]{2,1,0:T(8,128)S(1)} %get-tuple-element.110), channel_id=1, source_target_pairs={{1,2},{5,6},{9,10},{13,14},{17,18},{21,22},{25,26},{29,30},{0,4},{... | collective-permute-start | bytes 393224 | tf_op jit(solution)/shard_map/ppermute | solution.py:379
  37.2 11.5 %all-to-all-start.2 = ((f32[32,1,128]{2,1,0:T(1,128)}), f32[32,1,128]{2,1,0:T(1,128)S(1)}, u32[]{:S(2)}, u32[]{:S(2)}) async-start(f32[32,1,128]{2,1,0:T(1,128)} %broadcast_in_dim.41), calls=%async_computation.2 | async-start | bytes 32768 | tf_op jit(solution)/shard_map/all_to_all | solution.py:436
  49.8 6.2 %collective-permute-start.12 = (f32[8,8,1024]{2,1,0:T(8,128)S(1)}, f32[8,8,1024]{2,1,0:T(8,128)S(1)}, u32[]{:S(2)}, u32[]{:S(2)}) collective-permute-start(f32[8,8,1024]{2,1,0:T(8,128)S(1)} %get-tuple-element.123), channel_id=1, source_target_pairs={{0,4},{1,5},{2,6},{3,7},{8,12},{9,13},{10,14},{11,15},{16,20},{17,... | collective-permute-start | bytes 786440 | tf_op jit(solution)/shard_map/ppermute | solution.py:379
  49.8 9.3 %collective-permute-start.13 = (f32[8,8,1024]{2,1,0:T(8,128)S(1)}, f32[8,8,1024]{2,1,0:T(8,128)S(1)}, u32[]{:S(2)}, u32[]{:S(2)}) collective-permute-start(f32[8,8,1024]{2,1,0:T(8,128)S(1)} %get-tuple-element.124), channel_id=1, source_target_pairs={{4,8},{5,9},{6,10},{7,11},{12,16},{13,17},{14,18},{15,19},{20,24},... | collective-permute-start | bytes 786440 | tf_op jit(solution)/shard_map/ppermute | solution.py:379
  50.5 5.5 %collective-permute-start.14 = (f32[4,8,1024]{2,1,0:T(8,128)S(1)}, f32[4,8,1024]{2,1,0:T(8,128)S(1)}, u32[]{:S(2)}, u32[]{:S(2)}) collective-permute-start(f32[4,8,1024]{2,1,0:T(8,128)S(1)} %get-tuple-element.125), channel_id=1, source_target_pairs={{0,1},{2,3},{4,5},{6,7},{8,9},{10,11},{12,13},{14,15},{16,17},{18,... | collective-permute-start | bytes 393224 | tf_op jit(solution)/shard_map/ppermute | solution.py:379
  51.0 5.0 %collective-permute-start.15 = (f32[4,8,1024]{2,1,0:T(8,128)S(1)}, f32[4,8,1024]{2,1,0:T(8,128)S(1)}, u32[]{:S(2)}, u32[]{:S(2)}) collective-permute-start(f32[4,8,1024]{2,1,0:T(8,128)S(1)} %get-tuple-element.126), channel_id=1, source_target_pairs={{1,2},{5,6},{9,10},{13,14},{17,18},{21,22},{25,26},{29,30},{0,4},{... | collective-permute-start | bytes 393224 | tf_op jit(solution)/shard_map/ppermute | solution.py:379
  51.6 11.5 %all-to-all-start.3 = ((f32[32,1,128]{2,1,0:T(1,128)}), f32[32,1,128]{2,1,0:T(1,128)S(1)}, u32[]{:S(2)}, u32[]{:S(2)}) async-start(f32[32,1,128]{2,1,0:T(1,128)} %broadcast_in_dim.43), calls=%async_computation.3 | async-start | bytes 32768 | tf_op jit(solution)/shard_map/all_to_all | solution.py:436
